TPU v7x, 32 devices: a whole 2x2x4 slice. The times are simulated.
32 devices in a mesh: dp: 8 (over z, x), seq: 4 (over y, core).
Axes of the slice: x: 2, y: 2, z: 4, core: 2. Of those that a mesh axis runs over, the one named last changes fastest.
Arguments:
- caption_tokens: bfloat16 [128, 128, 768], P(('dp', 'seq')), may hold values from -6 to 6
- image_tokens: bfloat16 [128, 196, 768], P(('dp', 'seq')), may hold values from -6 to 6
- caption_lengths: int32 [128], P(('dp', 'seq')), may hold values from 8 to 128, as said below
- caption_image: int32 [128], P('dp'), may hold values from 0 to 127, as said below
- norm_gain: bfloat16 [768, 3], P(('dp', 'seq')), may hold values from 0.099609375 to 1.8984375
- norm_bias: bfloat16 [768, 3], P(('dp', 'seq')), may hold values from -1.25 to 1.25
- self_packed: bfloat16 [768, 2304], P(('dp', 'seq')), may hold values from -0.21875 to 0.21875
- self_output: bfloat16 [768, 768], P(('dp', 'seq')), may hold values from -0.625 to 0.625
- cross_query: bfloat16 [768, 768], P(('dp', 'seq')), may hold values from -0.21875 to 0.21875
- cross_pair: bfloat16 [768, 1536], P(('dp', 'seq')), may hold values from -0.21875 to 0.21875
- cross_output: bfloat16 [768, 768], P(('dp', 'seq')), may hold values from -0.75 to 0.75
- expand_weight: bfloat16 [768, 3072], P(('dp', 'seq')), may hold values from -0.21875 to 0.21875
- reduce_weight: bfloat16 [3072, 768], P(('dp', 'seq')), may hold values from -0.109375 to 0.109375
- cotangent: bfloat16 [128, 128, 768], P(('dp', 'seq')), may hold values from -6 to 6
Outputs:
- caption_out: bfloat16 [128, 128, 768], P(('dp', 'seq'))
- caption_grad: bfloat16 [128, 128, 768], P(('dp', 'seq'))
- image_grad: bfloat16 [128, 196, 768], P(('dp', 'seq'))
- gain_grad: float32 [768, 3], P(('dp', 'seq'))
- bias_grad: float32 [768, 3], P(('dp', 'seq'))
- self_packed_grad: float32 [768, 2304], P(('dp', 'seq'))
- self_output_grad: float32 [768, 768], P(('dp', 'seq'))
- cross_query_grad: float32 [768, 768], P(('dp', 'seq'))
- cross_pair_grad: float32 [768, 1536], P(('dp', 'seq'))
- cross_output_grad: float32 [768, 768], P(('dp', 'seq'))
- expand_grad: float32 [768, 3072], P(('dp', 'seq'))
- reduce_grad: float32 [3072, 768], P(('dp', 'seq'))
Inputs may be any that keep to these rules, and one draw needn't show every extreme that they name: `caption_lengths`: each aligned block of 4 captions holds at least one caption of length 128. `caption_image`: A permutation of the image indices. Caption c and its image lie in the same aligned block of 16; of each aligned block of 4 captions exactly 1 has its image in each aligned block of 4 images of that group.
All inputs are finite; a program needn't handle non-finite values.
Results may differ from a plain program's by a relative error of at most 0.022.
Values may be sent and summed in bfloat16 or wider, within the bound.
No kernel may reach another device: no remote copies, remote signals or barrier semaphores. Data moves between devices by JAX's collectives and lax.ppermute only.
A program may use at most 192 MiB of HBM per device.

v0:
```python
import functools
import itertools
import math

import jax
import jax.numpy as jnp
from jax import lax
from jax.experimental import pallas as pl
from jax.experimental.pallas import tpu as pltpu
from jax.sharding import PartitionSpec as P

HEADS = 12
HEAD_DIM = 64


epsilon = 1e-05


TILE = 384
LANES = 128


def project(values, weight):
    flat_rows = values.reshape(-1, values.shape[-1])
    return jnp.dot(flat_rows, weight, preferred_element_type=jnp.float32).reshape(
        values.shape[:-1] + (weight.shape[1],)
    )


def project_back(values, weight):
    flat_rows = values.reshape(-1, values.shape[-1])
    result = lax.dot_general(
        flat_rows, weight, (((1,), (1,)), ((), ())), preferred_element_type=jnp.float32
    )
    return result.reshape(values.shape[:-1] + (weight.shape[0],))


def weight_grad(left_rows, right_rows):
    return lax.dot_general(
        left_rows.reshape(-1, left_rows.shape[-1]),
        right_rows.reshape(-1, right_rows.shape[-1]),
        (((0,), (0,)), ((), ())),
        preferred_element_type=jnp.float32,
    )


def layer_norm(values, gain, shift):
    centred = values - jnp.mean(values, axis=-1, keepdims=True)
    spread = jnp.mean(centred * centred, axis=-1, keepdims=True)
    inverse = lax.rsqrt(spread + epsilon)
    scaled = centred * inverse
    return (scaled * gain + shift, scaled, inverse)


def norm_back(grad_rows, scaled, inverse, gain):
    weighted = grad_rows * gain
    result = inverse * (
        weighted
        - jnp.mean(weighted, axis=-1, keepdims=True)
        - scaled * jnp.mean(weighted * scaled, axis=-1, keepdims=True)
    )
    flat_grad = grad_rows.reshape(-1, grad_rows.shape[-1])
    flat_scaled = scaled.reshape(-1, scaled.shape[-1])
    return (result, jnp.sum(flat_grad * flat_scaled, axis=0), jnp.sum(flat_grad, axis=0))


def dot(left, right, contract):
    return lax.dot_general(left, right, (contract, ((), ())), preferred_element_type=jnp.float32)


def ffn_body(rows_ref, grad_ref, expand_ref, reduce_ref, order_ref, out_ref, back_ref, rgrad_ref, egrad_ref, *, ratio):
    rows, grad = rows_ref[...], grad_ref[...]
    width = rows.shape[1]
    stacked = jnp.concatenate([reduce_ref[:, k * width : (k + 1) * width] for k in range(ratio)], axis=0)
    reduce = dot(order_ref[...], stacked, ((1,), (0,))).astype(jnp.bfloat16)
    expand = expand_ref[...]
    gate = dot(rows, expand, ((1,), (0,)))
    grad_hidden = dot(grad, reduce, ((1,), (1,)))
    share = 0.5 * (1.0 + lax.erf(gate * math.sqrt(0.5)))
    slope = share + gate * (jnp.exp(-0.5 * gate * gate) * (1.0 / math.sqrt(2.0 * math.pi)))
    hidden = (gate * share).astype(jnp.bfloat16)
    grad_gate = (grad_hidden * slope).astype(jnp.bfloat16)
    rgrad_ref[...] = dot(hidden, grad, ((0,), (0,))).astype(jnp.bfloat16)
    egrad_ref[...] = dot(rows, grad_gate, ((0,), (0,))).astype(jnp.bfloat16)
    first = pl.program_id(0) == 0
    @pl.when(first)
    def _():
        out_ref[...] = jnp.zeros_like(out_ref)
        back_ref[...] = jnp.zeros_like(back_ref)
    out_ref[...] += dot(hidden, reduce, ((1,), (0,)))
    back_ref[...] += dot(grad_gate, expand, ((1,), (1,)))


def ffn(rows, grad, others, per_device, hidden_width):
    count, width = rows.shape
    ratio = hidden_width // width
    part = TILE // ratio
    place = jnp.arange(TILE)
    chunk = per_device * ratio
    source = part * (place % chunk // per_device) + per_device * (place // chunk) + place % per_device
    order = (source[:, None] == place[None, :]).astype(jnp.bfloat16)
    whole = lambda shape: pl.BlockSpec(shape, lambda j: (0, 0))
    return pl.pallas_call(
        functools.partial(ffn_body, ratio=ratio),
        grid=(hidden_width // TILE,),
        in_specs=[
            whole((count, width)), whole((count, width)),
            pl.BlockSpec((width, TILE), lambda j: (0, hidden_width // TILE + j)),
            pl.BlockSpec((part, hidden_width), lambda j: (j, 0)),
            whole((TILE, TILE)),
        ],
        out_specs=[
            whole((count, width)), whole((count, width)),
            pl.BlockSpec((TILE, width), lambda j: (j, 0)),
            pl.BlockSpec((width, TILE), lambda j: (0, j)),
        ],
        out_shape=[
            jax.ShapeDtypeStruct((count, width), jnp.float32),
            jax.ShapeDtypeStruct((count, width), jnp.float32),
            jax.ShapeDtypeStruct((hidden_width, width), jnp.bfloat16),
            jax.ShapeDtypeStruct((width, hidden_width), jnp.bfloat16),
        ],
        compiler_params=pltpu.CompilerParams(dimension_semantics=("arbitrary",), vmem_limit_bytes=48 << 20),
        name="ffn",
    )(rows, grad, others, others, order)


def stack_heads(block):
    left = lax.broadcasted_iota(jnp.int32, block.shape, 1) < HEAD_DIM
    none = jnp.zeros_like(block)
    return jnp.concatenate([jnp.where(left, block, none), jnp.where(left, none, block)], axis=0)


def join_heads(stacked):
    count = stacked.shape[0] // 2
    left = lax.broadcasted_iota(jnp.int32, (count, LANES), 1) < HEAD_DIM
    return jnp.where(left, stacked[:count], stacked[count:])


def pair_probs(query, key, length):
    scores = dot(key, query, ((1,), (1,)))
    if length is not None:
        row = lax.broadcasted_iota(jnp.int32, scores.shape, 0)
        column = lax.broadcasted_iota(jnp.int32, scores.shape, 1) % (scores.shape[1] // 2)
        scores = jnp.where((row <= column) & (row < length), scores, -1e30)
    spread = jnp.exp(scores - jnp.max(scores, axis=0, keepdims=True))
    return spread * (1.0 / jnp.sum(spread, axis=0, keepdims=True))


def scaled(block):
    return block * jnp.asarray(1.0 / math.sqrt(HEAD_DIM), block.dtype)


def attend_body(table_ref, query_ref, key_ref, value_ref, out_ref, *, causal):
    length = table_ref[pl.program_id(0)] if causal else None
    for start in range(0, HEADS * HEAD_DIM, LANES):
        lanes = slice(start, start + LANES)
        query = stack_heads(scaled(query_ref[0, :, lanes]))
        probs = pair_probs(query, key_ref[0, :, lanes], length).astype(jnp.bfloat16)
        out_ref[0, :, lanes] = join_heads(dot(probs, value_ref[0, :, lanes], ((0,), (0,)))).astype(jnp.bfloat16)


def attend_back_body(table_ref, query_ref, key_ref, value_ref, grad_ref, query_grad_ref, pair_grad_ref, *, causal):
    length = table_ref[pl.program_id(0)] if causal else None
    width = HEADS * HEAD_DIM
    for start in range(0, width, LANES):
        lanes = slice(start, start + LANES)
        query = stack_heads(scaled(query_ref[0, :, lanes]))
        grad = stack_heads(grad_ref[0, :, lanes])
        key, value = key_ref[0, :, lanes], value_ref[0, :, lanes]
        probs = pair_probs(query, key, length)
        grad_probs = dot(value, grad, ((1,), (1,)))
        grad_scores = probs * (grad_probs - jnp.sum(grad_probs * probs, axis=0, keepdims=True))
        grad_scores = grad_scores.astype(jnp.bfloat16)
        back = lambda left, right: dot(left, right, ((1,), (0,))).astype(jnp.bfloat16)
        grad_query = scaled(join_heads(dot(grad_scores, key, ((0,), (0,))))).astype(jnp.bfloat16)
        grad_key, grad_value = back(grad_scores, query), back(probs.astype(jnp.bfloat16), grad)
        query_grad_ref[0, :, lanes] = grad_query
        if causal:
            query_grad_ref[0, :, slice(width + start, width + start + LANES)] = grad_key
            query_grad_ref[0, :, slice(2 * width + start, 2 * width + start + LANES)] = grad_value
        else:
            pair_grad_ref[0, :, lanes] = grad_key
            pair_grad_ref[0, :, slice(width + start, width + start + LANES)] = grad_value


def attention(body, table, arrays, outs, name, heavy, routed=False):
    width = HEADS * HEAD_DIM
    captions = arrays[0][0].shape[0]
    own = arrays[0][0].shape[1]

    def spec(rows, cols, at):
        if routed and rows != own:
            return pl.BlockSpec((1, rows, cols), lambda c, place: (place[c], 0, at))
        return pl.BlockSpec((1, rows, cols), lambda c, place: (c, 0, at))

    work = heavy * 2 * captions * arrays[0][0].shape[1] * arrays[1][0].shape[1] * width
    return pl.pallas_call(
        body,
        grid_spec=pltpu.PrefetchScalarGridSpec(
            num_scalar_prefetch=1,
            grid=(captions,),
            in_specs=[spec(array.shape[1], width, at) for array, at in arrays],
            out_specs=[spec(rows, cols, 0) for rows, cols in outs],
        ),
        out_shape=[jax.ShapeDtypeStruct((captions, rows, cols), jnp.bfloat16) for rows, cols in outs],
        compiler_params=pltpu.CompilerParams(dimension_semantics=("arbitrary",), vmem_limit_bytes=48 << 20),
        cost_estimate=pl.CostEstimate(flops=work, transcendentals=0, bytes_accessed=0),
        name=name,
    )(table, *(array for array, _ in arrays))


def self_forward(packed, lengths):
    rows, width = packed.shape[1], HEADS * HEAD_DIM
    return attention(functools.partial(attend_body, causal=True), lengths,
        [(packed, 0), (packed, 1), (packed, 2)], [(rows, width)], "self_attention", 2)[0]


def cross_forward(query_rows, pair, place):
    return attention(functools.partial(attend_body, causal=False), place,
        [(query_rows, 0), (pair, 0), (pair, 1)], [query_rows.shape[1:]], "cross_attention", 2, True)[0]


def self_body(*refs):
    attend_back_body(*refs, None, causal=True)


def self_backward(packed, grad_rows, lengths):
    return attention(self_body, lengths,
        [(packed, 0), (packed, 1), (packed, 2), (grad_rows, 0)], [packed.shape[1:]], "self_backward", 5)[0]


def cross_backward(query_rows, pair, grad_rows, place):
    return attention(functools.partial(attend_back_body, causal=False), place,
        [(query_rows, 0), (pair, 0), (pair, 1), (grad_rows, 0)],
        [query_rows.shape[1:], pair.shape[1:]], "cross_backward", 5, True)


def index_bits():
    found = []
    for axis in ("dp", "seq"):
        count = lax.axis_size(axis)
        found += [(axis, bit) for bit in reversed(range(count.bit_length() - 1))]
    return found


def swap_pairs(axis, bit):
    return [(i, i ^ (1 << bit)) for i in range(lax.axis_size(axis))]


def own_bit(axis, bit):
    return (lax.axis_index(axis) >> bit) & 1


def gather_order(flip):
    far = [("dp", bit) for bit in range(1, lax.axis_size("dp").bit_length() - 1)][::-1]
    near = [[("dp", 0)], [("seq", bit) for bit in range(1, lax.axis_size("seq").bit_length() - 1)]]
    if flip:
        near = near[::-1]
    return far + near[0] + near[1] + [("seq", 0)]


class Gather:
    def __init__(self, part, flip):
        bits = index_bits()
        self.own = [own_bit(*place) for place in bits]
        self.known = [1] * len(bits)
        self.shape = part.shape
        self.piece = part.reshape((1,) * len(bits) + part.shape)
        self.whole = jnp.zeros((2,) * len(bits) + part.shape, part.dtype)
        self.whole = self.put(self.piece, self.own)
        self.left = gather_order(flip)

    def put(self, piece, starts):
        return lax.dynamic_update_slice(self.whole, piece, starts + [0] * len(self.shape))

    def starts(self):
        return [0 if size == 2 else bit for size, bit in zip(self.known, self.own)]

    def step(self):
        place = self.left.pop(0)
        dim = index_bits().index(place)
        starts = self.starts()
        if self.piece is None:
            self.piece = lax.dynamic_slice(
                self.whole, starts + [0] * len(self.shape), self.known + list(self.shape)
            )
        other = lax.ppermute(self.piece, place[0], swap_pairs(*place))
        starts[dim] = 1 - self.own[dim]
        self.whole = self.put(other, starts)
        self.known[dim] = 2
        self.piece = None

    def rows(self):
        return self.whole.reshape((-1,) + self.shape[1:])


class Scatter:
    def __init__(self, whole, flip, span):
        bits = index_bits()
        self.rows = whole.shape[0] >> len(bits)
        self.tail = whole.shape[1:]
        self.state = whole.reshape((2,) * len(bits) + (self.rows,) + self.tail)
        order = gather_order(flip)
        far = [place for place in order[:-3]][::-1]
        pairs = [far[i : i + span] for i in range(0, len(far), span)]
        self.left = [[order[-1]], [order[-2]], [order[-3]]] + pairs

    def part(self, places, turn):
        part = self.state
        for place, flipped in zip(places, turn):
            dim = index_bits().index(place)
            part = lax.dynamic_slice_in_dim(part, own_bit(*place) ^ flipped, 1, dim)
        return part

    def step(self):
        places = self.left.pop(0)
        axis = places[0][0]
        total = self.part(places, [0] * len(places))
        for turn in list(itertools.product((0, 1), repeat=len(places)))[1:]:
            mask = sum(flipped << place[1] for place, flipped in zip(places, turn))
            pairs = [(i, i ^ mask) for i in range(lax.axis_size(axis))]
            total = total + lax.ppermute(self.part(places, turn), axis, pairs)
        self.state = total

    def join(self, other):
        self.state = jnp.concatenate([self.state, other.state], axis=-1)
        self.tail = self.state.shape[-1:]

    def finish(self):
        while self.left:
            self.step()
        return self.state.reshape((self.rows,) + self.tail).astype(jnp.float32)


def advance(scatters, *values):
    held = lax.optimization_barrier(tuple(one.state for one in scatters) + values)
    for one, state in zip(scatters, held):
        one.state = state
        if one.left:
            one.step()
    values = held[len(scatters) :]
    return values[0] if len(values) == 1 else values


def swap(rows, k):
    if not k:
        return rows
    return lax.ppermute(rows, "seq", [(i, i ^ k) for i in range(lax.axis_size("seq"))])


def lay_body(*refs):
    start = 0
    for ref in refs[:-1]:
        refs[-1][:, start : start + ref.shape[1]] = ref[...]
        start += ref.shape[1]


def lay_side_by_side(pieces):
    width = sum(piece.shape[1] for piece in pieces)
    return pl.pallas_call(
        lay_body,
        out_shape=jax.ShapeDtypeStruct((pieces[0].shape[0], width), pieces[0].dtype),
        name="lay_side_by_side",
    )(*pieces)


def put_body(table_ref, *refs):
    for k, ref in enumerate(refs[:-1]):

        @pl.when(pl.program_id(0) == k)
        def _():
            refs[-1][...] = ref[...]


def put_rows(pieces, table):
    shape = pieces[0].shape
    return pl.pallas_call(
        put_body,
        grid_spec=pltpu.PrefetchScalarGridSpec(
            num_scalar_prefetch=1,
            grid=(len(pieces),),
            in_specs=[pl.BlockSpec(shape, lambda k, at: (0, 0, 0)) for _ in pieces],
            out_specs=pl.BlockSpec(shape, lambda k, at: (at[k], 0, 0)),
        ),
        out_shape=jax.ShapeDtypeStruct((len(pieces),) + shape[1:], pieces[0].dtype),
        compiler_params=pltpu.CompilerParams(dimension_semantics=("arbitrary",)),
        cost_estimate=pl.CostEstimate(
            flops=0, transcendentals=0, bytes_accessed=4 * len(pieces) * shape[1] * shape[2]
        ),
        name="put_rows",
    )(table, *pieces)


def shards(
    caption_tokens,
    image_tokens,
    caption_lengths,
    caption_image,
    norm_gain,
    norm_bias,
    self_packed,
    self_output,
    cross_query,
    cross_pair,
    cross_output,
    expand_weight,
    reduce_weight,
    cotangent,
):
    captions, seq_len, model_width = caption_tokens.shape
    peer_count = lax.axis_size("seq")
    position = lax.axis_index("seq")

    owner = (caption_image // captions % peer_count).reshape(peer_count, captions)
    slot = (caption_image % captions).reshape(peer_count, captions)
    peers = jnp.arange(peer_count)
    mine = (peers == position).astype(jnp.int32)
    place = jnp.sum(owner * mine[:, None], axis=0) ^ position
    asked = jnp.sum(jnp.where(owner == position, slot, 0), axis=1)
    turned = (peers[:, None] ^ position) == peers[None, :]
    asked = jnp.sum(jnp.where(turned, asked[None, :], 0), axis=1)
    paired = jnp.concatenate(
        [
            swap(lax.dynamic_slice_in_dim(image_tokens, asked[k], 1), k)
            for k in range(peer_count)
        ]
    )

    norm_columns = jnp.pad(jnp.concatenate([norm_gain, norm_bias], axis=1), ((0, 0), (0, 122)))
    rows = self_packed.shape[0]
    ratio = reduce_weight.shape[0] // rows
    reduce_blocks = [reduce_weight[k * rows : (k + 1) * rows] for k in range(ratio)]
    wide = lax.all_gather(
        lay_side_by_side(
            reduce_blocks + [expand_weight, cross_pair, self_output, cross_query, cross_output]
        ),
        ("dp", "seq"),
        axis=0,
        tiled=True,
    )
    first_group = Gather(jnp.concatenate([self_packed, norm_columns], axis=1), False)
    while first_group.left:
        first_group.step()
    first_group = first_group.rows()
    packed_weight = first_group[:, : 3 * model_width]
    norm_values = first_group[:, 3 * model_width : 3 * model_width + 6].astype(jnp.float32)
    norm_gains, norm_shifts = norm_values[:, :3], norm_values[:, 3:]
    hidden_width = expand_weight.shape[1]
    narrower = wide[:, 2 * hidden_width :]
    pair_weight = narrower[:, : 2 * model_width]
    output_weight = narrower[:, 2 * model_width : 3 * model_width]
    query_weight = narrower[:, 3 * model_width : 4 * model_width]
    cross_weight = narrower[:, 4 * model_width :]

    live_rows = jnp.arange(seq_len)[None, :] < caption_lengths[:, None]
    inputs = caption_tokens.astype(jnp.float32)
    normed_full, scaled_one, inverse_one = layer_norm(inputs, norm_gains[:, 0], norm_shifts[:, 0])
    normed_one = normed_full.astype(jnp.bfloat16)
    packed = project(normed_one, packed_weight).astype(jnp.bfloat16)
    attended = self_forward(packed, caption_lengths)
    after_self = inputs + project(attended, output_weight)
    normed_full_two, scaled_two, inverse_two = layer_norm(
        after_self, norm_gains[:, 1], norm_shifts[:, 1]
    )
    normed_two = normed_full_two.astype(jnp.bfloat16)
    image_pair = project(paired, pair_weight).astype(jnp.bfloat16)
    query_rows = project(normed_two, query_weight).astype(jnp.bfloat16)
    mixed_rows = cross_forward(query_rows, image_pair, place)
    branch = project(mixed_rows, cross_weight).astype(jnp.bfloat16)
    after_cross = after_self + branch.astype(jnp.float32)
    normed_full_three, scaled_three, inverse_three = layer_norm(
        after_cross, norm_gains[:, 2], norm_shifts[:, 2]
    )
    normed_three = normed_full_three.astype(jnp.bfloat16)
    grad_out = jnp.where(live_rows[..., None], cotangent, jnp.zeros_like(cotangent))
    flat = lambda member: member.reshape(-1, model_width)
    forward, backward, reduce_part, expand_part = ffn(
        flat(normed_three), flat(grad_out), wide, rows, hidden_width
    )
    caption_out = jnp.where(
        live_rows[..., None], after_cross + forward.reshape(after_cross.shape), 0.0
    ).astype(jnp.bfloat16)

    narrow = lambda member: member.astype(jnp.bfloat16)
    reduce_sums = Scatter(reduce_part, True, 1)
    expand_sums = Scatter(expand_part, False, 1)
    reduce_sums.step()
    expand_sums.step()
    grad_norm_three, gain_three, shift_three = norm_back(
        backward.reshape(after_cross.shape), scaled_three, inverse_three, norm_gains[:, 2]
    )
    grad_second = grad_out.astype(jnp.float32) + grad_norm_three
    grad_branch = grad_second.astype(jnp.bfloat16)
    grad_cross_mixed = project_back(grad_branch, cross_weight).astype(jnp.bfloat16)
    grad_cross_mixed, grad_branch = advance(
        [reduce_sums, expand_sums], grad_cross_mixed, grad_branch
    )
    cross_output_grad = weight_grad(mixed_rows, grad_branch)
    grad_cross_rows, grad_pair = cross_backward(
        query_rows, image_pair, grad_cross_mixed, place
    )
    cross_pair_grad = weight_grad(paired, grad_pair)
    cross_sums = Scatter(
        narrow(jnp.concatenate([cross_pair_grad, cross_output_grad], axis=1)), True, 2
    )
    grad_pair, grad_cross_rows = advance(
        [reduce_sums, expand_sums, cross_sums], grad_pair, grad_cross_rows
    )
    image_rows = project_back(grad_pair, pair_weight).astype(jnp.bfloat16)
    cross_query_grad = weight_grad(normed_two, grad_cross_rows)
    grad_norm_two, gain_two, shift_two = norm_back(
        project_back(grad_cross_rows, query_weight).astype(jnp.bfloat16).astype(jnp.float32),
        scaled_two,
        inverse_two,
        norm_gains[:, 1],
    )
    grad_first = grad_second + grad_norm_two
    grad_self = grad_first.astype(jnp.bfloat16)
    self_output_grad = weight_grad(attended, grad_self)
    grad_self, image_rows = advance([reduce_sums, expand_sums, cross_sums], grad_self, image_rows)
    home = [swap(image_rows[k : k + 1], k) for k in range(peer_count)]
    grad_attended = project_back(grad_self, output_weight).astype(jnp.bfloat16)
    grad_packed = self_backward(packed, grad_attended, caption_lengths)
    grad_packed, *home = advance([reduce_sums, expand_sums, cross_sums], grad_packed, *home)
    self_packed_grad = weight_grad(normed_one, grad_packed)
    grad_norm_one, gain_one, shift_one = norm_back(
        project_back(grad_packed, packed_weight), scaled_one, inverse_one, norm_gains[:, 0]
    )
    caption_grad = (grad_first + grad_norm_one).astype(jnp.bfloat16)
    norm_sums = jnp.stack([gain_one, gain_two, gain_three, shift_one, shift_two, shift_three], axis=1)
    half = model_width // 2
    left = jnp.concatenate([cross_query_grad, self_output_grad, self_packed_grad[:, :half]], axis=1)
    right = jnp.concatenate(
        [self_packed_grad[:, half:], jnp.pad(norm_sums, ((0, 0), (0, 122)))], axis=1
    )
    left_sums = Scatter(narrow(left), True, 2)
    right_sums = Scatter(narrow(right), False, 2)
    left_sums.step()
    right_sums.step()
    groups = [cross_sums, reduce_sums, expand_sums, left_sums, right_sums]
    while len(left_sums.left) > 1:
        advance(groups)
    left_sums.join(right_sums)
    home = advance([left_sums], *home)
    image_grad = put_rows(list(home), asked)
    self_sums = left_sums.finish()
    reduce_grad, expand_grad = reduce_sums.finish(), expand_sums.finish()
    cross_sums = cross_sums.finish()
    last = 5 * model_width
    return (
        caption_out,
        caption_grad,
        image_grad,
        self_sums[:, last : last + 3],
        self_sums[:, last + 3 : last + 6],
        self_sums[:, 2 * model_width : last],
        self_sums[:, model_width : 2 * model_width],
        self_sums[:, :model_width],
        cross_sums[:, : 2 * model_width],
        cross_sums[:, 2 * model_width :],
        expand_grad,
        reduce_grad,
    )


def solution(mesh):
    placed = (
        P(("dp", "seq"), None, None),
        P(("dp", "seq"), None, None),
        P(("dp", "seq")),
        P("dp"),
        P(("dp", "seq"), None),
        P(("dp", "seq"), None),
        P(("dp", "seq"), None),
        P(("dp", "seq"), None),
        P(("dp", "seq"), None),
        P(("dp", "seq"), None),
        P(("dp", "seq"), None),
        P(("dp", "seq"), None),
        P(("dp", "seq"), None),
        P(("dp", "seq"), None, None),
    )
    return jax.shard_map(
        shards,
        mesh=mesh,
        in_specs=placed,
        out_specs=(
            P(("dp", "seq"), None, None),
            P(("dp", "seq"), None, None),
            P(("dp", "seq"), None, None),
            P(("dp", "seq"), None),
            P(("dp", "seq"), None),
            P(("dp", "seq"), None),
            P(("dp", "seq"), None),
            P(("dp", "seq"), None),
            P(("dp", "seq"), None),
            P(("dp", "seq"), None),
            P(("dp", "seq"), None),
            P(("dp", "seq"), None),
        ),
        check_vma=False,
    )
```

profile of v0, /device:TPU:0, one launch (start us, length us, event | category | flops | bytes accessed | tf_op | source)
XLA Modules:
  0.0 389.3 jit_solution(11163254048505445168)
XLA Ops:
  10.8 4.1 %collective-permute-start = (bf16[1,1,1,1,1,24,2432]{6,5,4,3,2,1,0:T(8,128)(2,1)S(1)}, bf16[1,1,1,1,1,24,2432]{6,5,4,3,2,1,0:T(8,128)(2,1)S(1)}, u32[]{:S(2)}, u32[]{:S(2)}) collective-permute-start(bf16[1,1,1,1,1,24,2432]{6,5,4,3,2,1,0:T(8,128)(2,1)S(1)} %fusion.25), channel_id=1, source_target_pairs={{0,16},{4,20},{8,24},{12,28},{16,0},{20,4},{24,8},{28,12},{1,17},{... | collective-permute-start | bytes 350216 | tf_op jit(solution)/shard_map/ppermute | solution.py:288
  17.7 3.0 collective-permute-done
  23.0 11.5 %collective-permute-done.1 = bf16[2,1,1,1,1,24,2432]{6,5,4,3,2,1,0:T(8,128)(2,1)S(1)} collective-permute-done((bf16[2,1,1,1,1,24,2432]{6,5,4,3,2,1,0:T(8,128)(2,1)S(1)}, bf16[2,1,1,1,1,24,2432]{6,5,4,3,2,1,0:T(8,128)(2,1)S(1)}, u32[]{:S(2)}, u32[]{:S(2)}) %collective-permute-start.1) | collective-permute-done | bytes 233504 | tf_op jit(solution)/shard_map/ppermute | solution.py:288
  37.9 8.0 %collective-permute-done.2 = bf16[2,2,1,1,1,24,2432]{6,5,4,3,2,1,0:T(8,128)(2,1)S(1)} collective-permute-done((bf16[2,2,1,1,1,24,2432]{6,5,4,3,2,1,0:T(8,128)(2,1)S(1)}, bf16[2,2,1,1,1,24,2432]{6,5,4,3,2,1,0:T(8,128)(2,1)S(1)}, u32[]{:S(2)}, u32[]{:S(2)}) %collective-permute-start.2) | collective-permute-done | bytes 466976 | tf_op jit(solution)/shard_map/ppermute | solution.py:288
  64.4 12.8 %collective-permute-done.3 = bf16[2,2,2,1,1,24,2432]{6,5,4,3,2,1,0:T(8,128)(2,1)S(1)} collective-permute-done((bf16[2,2,2,1,1,24,2432]{6,5,4,3,2,1,0:T(8,128)(2,1)}, bf16[2,2,2,1,1,24,2432]{6,5,4,3,2,1,0:T(8,128)(2,1)S(1)}, u32[]{:S(2)}, u32[]{:S(2)}) %collective-permute-start.3) | collective-permute-done | bytes 933920 | tf_op jit(solution)/shard_map/ppermute | solution.py:288
  78.2 3.0 constant_dynamic-slice_fusion.28
  85.9 4.8 %collective-permute-done.7 = bf16[1,196,768]{2,1,0:T(8,128)(2,1)} collective-permute-done((bf16[1,196,768]{2,1,0:T(8,128)(2,1)S(1)}, bf16[1,196,768]{2,1,0:T(8,128)(2,1)}, u32[]{:S(2)}, u32[]{:S(2)}) %collective-permute-start.7) | collective-permute-done | bytes 301088 | tf_op jit(solution)/shard_map/ppermute | solution.py:349
  91.8 3.4 constant_dynamic-update-slice_fusion
  97.4 4.2 %convolution_convert_fusion.query_ref.key_ref.value_ref.refs_1_.refs_2_.refs_3_ = bf16[4,128,2304]{2,1,0:T(8,128)(2,1)S(1)} fusion(bf16[768,2432]{1,0:T(8,128)(2,1)} %bitcast.1, f32[768]{0:T(1024)S(1)} %get-tuple-element.159, f32[768]{0:T(1024)S(1)} %get-tuple-element.160, f32[4,128]{1,0:T(4,128)S(1)} %add_rsqrt_fusion.2, ...), kind=kOutput, calls=%fused_computation.2 | convolution fusion | flops 1815478272 | bytes 6694912 | tf_op jit(solution)/shard_map/dot_general | solution.py:25
  101.6 4.5 %self_attention.1 = bf16[4,128,768]{2,1,0:T(8,128)(2,1)S(1)} custom-call(s32[4]{0:T(128)S(1)} %copy-done.10, bf16[4,128,2304]{2,1,0:T(8,128)(2,1)S(1)} %convolution_convert_fusion.query_ref.key_ref.value_ref.refs_1_.refs_2_.refs_3_, bf16[4,128,2304]{2,1,0:T(8,128)(2,1)S(1)} %convolution_convert_fusion.query_ref.key_ref.value_ref.refs_1_.refs_2_.refs_3_, ...), custom_call_target="tpu_custom_call" | custom-call | flops 201326592 | tf_op jit(solution)/shard_map/self_attention/pallas_call | solution.py:198
  106.1 30.4 %all-gather.2.cloned.1.call-done.expand_ref.reduce_ref = bf16[768,9984]{1,0:T(8,128)(2,1)} async-done(((bf16[24,9984]{1,0:T(8,128)(2,1)}), bf16[768,9984]{1,0:T(8,128)(2,1)}) %all-gather.2.cloned.1.call-update) | async-done | bytes 15335440 | tf_op jit(solution)/shard_map/all_gather | solution.py:434
  140.7 3.7 convolution_convert_fusion.1.key_ref.value_ref
  144.4 3.1 convolution_convert_fusion.6.query_ref
  147.5 4.1 %cross_attention.1 = bf16[4,128,768]{2,1,0:T(8,128)(2,1)S(1)} custom-call(s32[4]{0:T(128)S(1)} %broadcast_xor_fusion.table_ref, bf16[4,128,768]{2,1,0:T(8,128)(2,1)S(1)} %convolution_convert_fusion.6.query_ref, bf16[4,196,1536]{2,1,0:T(8,128)(2,1)S(1)} %convolution_convert_fusion.1.key_ref.value_ref, ...), custom_call_target="tpu_custom_call" | custom-call | flops 308281344 | tf_op jit(solution)/shard_map/cross_attention/pallas_call | solution.py:198
  155.8 25.7 %ffn.1 = (f32[512,768]{1,0:T(8,128)S(1)}, f32[512,768]{1,0:T(8,128)S(1)}, bf16[3072,768]{1,0:T(8,128)(2,1)}, bf16[768,3072]{1,0:T(8,128)(2,1)}) custom-call(bf16[512,768]{1,0:T(8,128)(2,1)S(1)} %bitcast.110, bf16[512,768]{1,0:T(8,128)(2,1)S(1)} %bitcast.109, bf16[768,9984]{1,0:T(8,128)(2,1)} %all-gather.2.cloned.1.call-done.expand_ref.reduce_ref, ...), custom_call_target="tpu_custom_call" | custom-call | tf_op jit(solution)/shard_map/ffn/pallas_call | solution.py:103
  181.5 4.4 %constant_dynamic-slice_fusion.23 = bf16[2,2,2,2,1,96,768]{6,5,4,3,2,1,0:T(8,128)(2,1)} fusion(bf16[2,2,2,2,2,96,768]{6,5,4,3,2,1,0:T(8,128)(2,1)} %bitcast.120, s32[]{:T(128)S(6)} %select_n.225), kind=kLoop, calls=%fused_computation.128 | loop fusion | bytes 4718596 | tf_op jit(solution)/shard_map/dynamic_slice | solution.py:313
  205.5 11.8 %cross_backward.1 = (bf16[4,128,768]{2,1,0:T(8,128)(2,1)S(1)}, bf16[4,196,1536]{2,1,0:T(8,128)(2,1)S(1)}) custom-call(s32[4]{0:T(128)S(1)} %broadcast_xor_fusion.table_ref, bf16[4,128,768]{2,1,0:T(8,128)(2,1)S(1)} %copy-done.4, bf16[4,196,1536]{2,1,0:T(8,128)(2,1)} %copy-done, bf16[4,196,1536]{2,1,0:T(8,128)(2,1)} %copy-done, ...), custom_call_target="tpu_custom_call" | custom-call | flops 770703360 | tf_op jit(solution)/shard_map/cross_backward/pallas_call | solution.py:198
  217.3 4.5 %bitcast_convert_fusion.1 = bf16[768,1536]{1,0:T(8,128)(2,1)S(1)} fusion(bf16[4,196,768]{2,1,0:T(8,128)(2,1)} %copy-done.53, bf16[4,196,1536]{2,1,0:T(8,128)(2,1)S(1)} %get-tuple-element.69), kind=kOutput, calls=%fused_computation.1 | convolution fusion | flops 1850867712 | bytes 5971968 | tf_op jit(solution)/shard_map/dot_general | solution.py:39
  222.9 8.0 %collective-permute-done.10 = bf16[2,2,1,2,1,96,768]{6,5,4,3,2,1,0:T(8,128)(2,1)} collective-permute-done((bf16[2,2,1,2,1,96,768]{6,5,4,3,2,1,0:T(8,128)(2,1)}, bf16[2,2,1,2,1,96,768]{6,5,4,3,2,1,0:T(8,128)(2,1)}, u32[]{:S(2)}, u32[]{:S(2)}) %collective-permute-start.10) | collective-permute-done | bytes 1179680 | tf_op jit(solution)/shard_map/ppermute | solution.py:323
  241.8 5.2 %fusion.21 = bf16[4,196,768]{2,1,0:T(8,128)(2,1)} fusion(bf16[4,196,1536]{2,1,0:T(8,128)(2,1)S(1)} %get-tuple-element.69, bf16[768,9984]{1,0:T(8,128)(2,1)} %all-gather.2.cloned.1.call-done.expand_ref.reduce_ref), kind=kOutput, calls=%fused_computation.58 | convolution fusion | flops 1850290176 | bytes 5971968 | tf_op jit(solution)/shard_map/dot_general | solution.py:32
  261.0 10.6 %collective-permute-start.15 = (bf16[2,1,1,1,1,96,768]{6,5,4,3,2,1,0:T(8,128)(2,1)S(1)}, bf16[2,1,1,1,1,96,768]{6,5,4,3,2,1,0:T(8,128)(2,1)S(1)}, u32[]{:S(2)}, u32[]{:S(2)}) collective-permute-start(bf16[2,1,1,1,1,96,768]{6,5,4,3,2,1,0:T(8,128)(2,1)S(1)} %constant_dynamic-slice_fusion.16), channel_id=1, source_target_pairs={{0,8},{4,12},{8,0},{12,4},{16,24},{20,28},{24,16},{28,20},{1,9},{5... | collective-permute-start | bytes 884744 | tf_op jit(solution)/shard_map/ppermute | solution.py:323
  276.3 8.7 %self_backward.1 = bf16[4,128,2304]{2,1,0:T(8,128)(2,1)S(1)} custom-call(s32[4]{0:T(128)S(1)} %copy-done.10, bf16[4,128,2304]{2,1,0:T(8,128)(2,1)S(1)} %convolution_convert_fusion.query_ref.key_ref.value_ref.refs_1_.refs_2_.refs_3_, bf16[4,128,2304]{2,1,0:T(8,128)(2,1)S(1)} %convolution_convert_fusion.query_ref.key_ref.value_ref.refs_1_.refs_2_.refs_3_, ...), custom_call_target="tpu_custom_call" | custom-call | flops 503316480 | tf_op jit(solution)/shard_map/self_backward/pallas_call | solution.py:198
  286.5 7.0 %collective-permute-done.17 = bf16[2,2,1,2,1,24,2304]{6,5,4,3,2,1,0:T(8,128)(2,1)S(1)} collective-permute-done((bf16[2,2,1,2,1,24,2304]{6,5,4,3,2,1,0:T(8,128)(2,1)S(1)}, bf16[2,2,1,2,1,24,2304]{6,5,4,3,2,1,0:T(8,128)(2,1)S(1)}, u32[]{:S(2)}, u32[]{:S(2)}) %collective-permute-start.17) | collective-permute-done | bytes 884768 | tf_op jit(solution)/shard_map/ppermute | solution.py:323
  299.3 4.0 %fusion.1 = f32[512,768]{1,0:T(8,128)S(1)} fusion(bf16[512,2304]{1,0:T(8,128)(2,1)S(1)} %bitcast.111, bf16[768,2432]{1,0:T(8,128)(2,1)} %bitcast.1), kind=kOutput, calls=%fused_computation.8 | convolution fusion | flops 1811939328 | bytes 7471104 | tf_op jit(solution)/shard_map/dot_general | solution.py:32
  308.0 3.0 collective-permute-start.22
  322.2 2.6 collective-permute-done.23
  341.4 10.0 %collective-permute-done.29 = bf16[2,2,1,2,1,24,1920]{6,5,4,3,2,1,0:T(8,128)(2,1)S(1)} collective-permute-done((bf16[2,2,1,2,1,24,1920]{6,5,4,3,2,1,0:T(8,128)(2,1)S(1)}, bf16[2,2,1,2,1,24,1920]{6,5,4,3,2,1,0:T(8,128)(2,1)S(1)}, u32[]{:S(2)}, u32[]{:S(2)}) %collective-permute-start.29) | collective-permute-done | bytes 737312 | tf_op jit(solution)/shard_map/ppermute | solution.py:323
  357.1 6.3 %collective-permute-done.31 = bf16[2,2,1,1,1,24,1920]{6,5,4,3,2,1,0:T(8,128)(2,1)S(1)} collective-permute-done((bf16[2,2,1,1,1,24,1920]{6,5,4,3,2,1,0:T(8,128)(2,1)S(1)}, bf16[2,2,1,1,1,24,1920]{6,5,4,3,2,1,0:T(8,128)(2,1)S(1)}, u32[]{:S(2)}, u32[]{:S(2)}) %collective-permute-start.31) | collective-permute-done | bytes 368672 | tf_op jit(solution)/shard_map/ppermute | solution.py:323
  365.6 2.6 collective-permute-start.33
  368.9 3.6 put_rows.1
  372.5 2.8 copy.77
  375.3 3.9 %collective-permute-done.33 = bf16[1,1,1,1,1,24,3968]{6,5,4,3,2,1,0:T(8,128)(2,1)S(1)} collective-permute-done((bf16[1,1,1,1,1,24,3968]{6,5,4,3,2,1,0:T(8,128)(2,1)S(1)}, bf16[1,1,1,1,1,24,3968]{6,5,4,3,2,1,0:T(8,128)(2,1)S(1)}, u32[]{:S(2)}, u32[]{:S(2)}) %collective-permute-start.33) | collective-permute-done | bytes 190496 | tf_op jit(solution)/shard_map/ppermute | solution.py:323
  (332 shorter events, 140.7 us)
Async XLA Ops:
  7.2 129.2 %all-gather.2.cloned.1.call-start = ((), (), s32[]{:S(2)}) async-start(), calls=%async_computation | async-start | bytes 15814656 | tf_op jit(solution)/shard_map/all_gather | solution.py:434
  10.8 9.8 %collective-permute-start = (bf16[1,1,1,1,1,24,2432]{6,5,4,3,2,1,0:T(8,128)(2,1)S(1)}, bf16[1,1,1,1,1,24,2432]{6,5,4,3,2,1,0:T(8,128)(2,1)S(1)}, u32[]{:S(2)}, u32[]{:S(2)}) collective-permute-start(bf16[1,1,1,1,1,24,2432]{6,5,4,3,2,1,0:T(8,128)(2,1)S(1)} %fusion.25), channel_id=1, source_target_pairs={{0,16},{4,20},{8,24},{12,28},{16,0},{20,4},{24,8},{28,12},{1,17},{... | collective-permute-start | bytes 350216 | tf_op jit(solution)/shard_map/ppermute | solution.py:288
  22.3 12.2 %collective-permute-start.1 = (bf16[2,1,1,1,1,24,2432]{6,5,4,3,2,1,0:T(8,128)(2,1)S(1)}, bf16[2,1,1,1,1,24,2432]{6,5,4,3,2,1,0:T(8,128)(2,1)S(1)}, u32[]{:S(2)}, u32[]{:S(2)}) collective-permute-start(bf16[2,1,1,1,1,24,2432]{6,5,4,3,2,1,0:T(8,128)(2,1)S(1)} %constant_dynamic-slice_fusion.31), channel_id=1, source_target_pairs={{0,8},{4,12},{8,0},{12,4},{16,24},{20,28},{24,16},{28,20},{1,9},{5... | collective-permute-start | bytes 700424 | tf_op jit(solution)/shard_map/ppermute | solution.py:288
  36.3 9.6 %collective-permute-start.2 = (bf16[2,2,1,1,1,24,2432]{6,5,4,3,2,1,0:T(8,128)(2,1)S(1)}, bf16[2,2,1,1,1,24,2432]{6,5,4,3,2,1,0:T(8,128)(2,1)S(1)}, u32[]{:S(2)}, u32[]{:S(2)}) collective-permute-start(bf16[2,2,1,1,1,24,2432]{6,5,4,3,2,1,0:T(8,128)(2,1)S(1)} %constant_dynamic-slice_fusion.30), channel_id=1, source_target_pairs={{0,4},{4,0},{8,12},{12,8},{16,20},{20,16},{24,28},{28,24},{1,5},{5... | collective-permute-start | bytes 1400840 | tf_op jit(solution)/shard_map/ppermute | solution.py:288
  49.0 28.2 %collective-permute-start.3 = (bf16[2,2,2,1,1,24,2432]{6,5,4,3,2,1,0:T(8,128)(2,1)}, bf16[2,2,2,1,1,24,2432]{6,5,4,3,2,1,0:T(8,128)(2,1)S(1)}, u32[]{:S(2)}, u32[]{:S(2)}) collective-permute-start(bf16[2,2,2,1,1,24,2432]{6,5,4,3,2,1,0:T(8,128)(2,1)} %constant_dynamic-slice_fusion.29), channel_id=1, source_target_pairs={{0,2},{1,3},{2,0},{3,1},{4,6},{5,7},{6,4},{7,5},{8,10},{9,11},{10,... | collective-permute-start | bytes 2801672 | tf_op jit(solution)/shard_map/ppermute | solution.py:288
  61.7 21.5 %collective-permute-start.5 = (bf16[1,196,768]{2,1,0:T(8,128)(2,1)}, bf16[1,196,768]{2,1,0:T(8,128)(2,1)}, u32[]{:S(2)}, u32[]{:S(2)}) collective-permute-start(bf16[1,196,768]{2,1,0:T(8,128)(2,1)} %copy.85), channel_id=1, source_target_pairs={{0,1},{1,0},{2,3},{3,2},{4,5},{5,4},{6,7},{7,6},{8,9},{9,8},{10,11... | collective-permute-start | bytes 903176 | tf_op jit(solution)/shard_map/ppermute | solution.py:349
  61.8 23.1 %collective-permute-start.6 = (bf16[1,196,768]{2,1,0:T(8,128)(2,1)S(1)}, bf16[1,196,768]{2,1,0:T(8,128)(2,1)}, u32[]{:S(2)}, u32[]{:S(2)}) collective-permute-start(bf16[1,196,768]{2,1,0:T(8,128)(2,1)S(1)} %copy.86), channel_id=1, source_target_pairs={{0,2},{1,3},{2,0},{3,1},{4,6},{5,7},{6,4},{7,5},{8,10},{9,11},{10,... | collective-permute-start | bytes 903176 | tf_op jit(solution)/shard_map/ppermute | solution.py:349
  63.0 27.7 %collective-permute-start.7 = (bf16[1,196,768]{2,1,0:T(8,128)(2,1)S(1)}, bf16[1,196,768]{2,1,0:T(8,128)(2,1)}, u32[]{:S(2)}, u32[]{:S(2)}) collective-permute-start(bf16[1,196,768]{2,1,0:T(8,128)(2,1)S(1)} %copy.87), channel_id=1, source_target_pairs={{0,3},{1,2},{2,1},{3,0},{4,7},{5,6},{6,5},{7,4},{8,11},{9,10},{10,... | collective-permute-start | bytes 903176 | tf_op jit(solution)/shard_map/ppermute | solution.py:349
  81.2 10.6 %collective-permute-start.4 = (bf16[2,2,2,2,1,24,2432]{6,5,4,3,2,1,0:T(8,128)(2,1)}, bf16[2,2,2,2,1,24,2432]{6,5,4,3,2,1,0:T(8,128)(2,1)}, u32[]{:S(2)}, u32[]{:S(2)}) collective-permute-start(bf16[2,2,2,2,1,24,2432]{6,5,4,3,2,1,0:T(8,128)(2,1)} %constant_dynamic-slice_fusion.28), channel_id=1, source_target_pairs={{0,1},{1,0},{2,3},{3,2},{4,5},{5,4},{6,7},{7,6},{8,9},{9,8},{10,11... | collective-permute-start | bytes 5603336 | tf_op jit(solution)/shard_map/ppermute | solution.py:288
  185.9 11.1 %collective-permute-start.8 = (bf16[2,2,2,2,1,96,768]{6,5,4,3,2,1,0:T(8,128)(2,1)}, bf16[2,2,2,2,1,96,768]{6,5,4,3,2,1,0:T(8,128)(2,1)}, u32[]{:S(2)}, u32[]{:S(2)}) collective-permute-start(bf16[2,2,2,2,1,96,768]{6,5,4,3,2,1,0:T(8,128)(2,1)} %constant_dynamic-slice_fusion.23), channel_id=1, source_target_pairs={{0,1},{1,0},{2,3},{3,2},{4,5},{5,4},{6,7},{7,6},{8,9},{9,8},{10,11... | collective-permute-start | bytes 7077896 | tf_op jit(solution)/shard_map/ppermute | solution.py:323
  187.8 11.3 %collective-permute-start.9 = (bf16[2,2,2,2,1,24,3072]{6,5,4,3,2,1,0:T(8,128)(2,1)}, bf16[2,2,2,2,1,24,3072]{6,5,4,3,2,1,0:T(8,128)(2,1)}, u32[]{:S(2)}, u32[]{:S(2)}) collective-permute-start(bf16[2,2,2,2,1,24,3072]{6,5,4,3,2,1,0:T(8,128)(2,1)} %constant_dynamic-slice_fusion.22), channel_id=1, source_target_pairs={{0,1},{1,0},{2,3},{3,2},{4,5},{5,4},{6,7},{7,6},{8,9},{9,8},{10,11... | collective-permute-start | bytes 7077896 | tf_op jit(solution)/shard_map/ppermute | solution.py:323
  202.3 28.6 %collective-permute-start.10 = (bf16[2,2,1,2,1,96,768]{6,5,4,3,2,1,0:T(8,128)(2,1)}, bf16[2,2,1,2,1,96,768]{6,5,4,3,2,1,0:T(8,128)(2,1)}, u32[]{:S(2)}, u32[]{:S(2)}) collective-permute-start(bf16[2,2,1,2,1,96,768]{6,5,4,3,2,1,0:T(8,128)(2,1)} %constant_dynamic-slice_fusion.21), channel_id=1, source_target_pairs={{0,4},{4,0},{8,12},{12,8},{16,20},{20,16},{24,28},{28,24},{1,5},{5... | collective-permute-start | bytes 3538952 | tf_op jit(solution)/shard_map/ppermute | solution.py:323
  205.4 28.1 %collective-permute-start.11 = (bf16[2,2,2,1,1,24,3072]{6,5,4,3,2,1,0:T(8,128)(2,1)}, bf16[2,2,2,1,1,24,3072]{6,5,4,3,2,1,0:T(8,128)(2,1)}, u32[]{:S(2)}, u32[]{:S(2)}) collective-permute-start(bf16[2,2,2,1,1,24,3072]{6,5,4,3,2,1,0:T(8,128)(2,1)} %constant_dynamic-slice_fusion.20), channel_id=1, source_target_pairs={{0,2},{1,3},{2,0},{3,1},{4,6},{5,7},{6,4},{7,5},{8,10},{9,11},{10,... | collective-permute-start | bytes 3538952 | tf_op jit(solution)/shard_map/ppermute | solution.py:323
  235.9 20.7 %collective-permute-start.12 = (bf16[2,2,1,1,1,96,768]{6,5,4,3,2,1,0:T(8,128)(2,1)}, bf16[2,2,1,1,1,96,768]{6,5,4,3,2,1,0:T(8,128)(2,1)}, u32[]{:S(2)}, u32[]{:S(2)}) collective-permute-start(bf16[2,2,1,1,1,96,768]{6,5,4,3,2,1,0:T(8,128)(2,1)} %constant_dynamic-slice_fusion.19), channel_id=1, source_target_pairs={{0,2},{1,3},{2,0},{3,1},{4,6},{5,7},{6,4},{7,5},{8,10},{9,11},{10,... | collective-permute-start | bytes 1769480 | tf_op jit(solution)/shard_map/ppermute | solution.py:323
  237.1 20.9 %collective-permute-start.13 = (bf16[2,2,1,1,1,24,3072]{6,5,4,3,2,1,0:T(8,128)(2,1)}, bf16[2,2,1,1,1,24,3072]{6,5,4,3,2,1,0:T(8,128)(2,1)}, u32[]{:S(2)}, u32[]{:S(2)}) collective-permute-start(bf16[2,2,1,1,1,24,3072]{6,5,4,3,2,1,0:T(8,128)(2,1)} %constant_dynamic-slice_fusion.18), channel_id=1, source_target_pairs={{0,4},{4,0},{8,12},{12,8},{16,20},{20,16},{24,28},{28,24},{1,5},{5... | collective-permute-start | bytes 1769480 | tf_op jit(solution)/shard_map/ppermute | solution.py:323
  239.4 19.8 %collective-permute-start.14 = (bf16[2,2,2,2,1,24,2304]{6,5,4,3,2,1,0:T(8,128)(2,1)}, bf16[2,2,2,2,1,24,2304]{6,5,4,3,2,1,0:T(8,128)(2,1)}, u32[]{:S(2)}, u32[]{:S(2)}) collective-permute-start(bf16[2,2,2,2,1,24,2304]{6,5,4,3,2,1,0:T(8,128)(2,1)} %constant_dynamic-slice_fusion.17), channel_id=1, source_target_pairs={{0,1},{1,0},{2,3},{3,2},{4,5},{5,4},{6,7},{7,6},{8,9},{9,8},{10,11... | collective-permute-start | bytes 5308424 | tf_op jit(solution)/shard_map/ppermute | solution.py:323
  261.0 24.1 %collective-permute-start.15 = (bf16[2,1,1,1,1,96,768]{6,5,4,3,2,1,0:T(8,128)(2,1)S(1)}, bf16[2,1,1,1,1,96,768]{6,5,4,3,2,1,0:T(8,128)(2,1)S(1)}, u32[]{:S(2)}, u32[]{:S(2)}) collective-permute-start(bf16[2,1,1,1,1,96,768]{6,5,4,3,2,1,0:T(8,128)(2,1)S(1)} %constant_dynamic-slice_fusion.16), channel_id=1, source_target_pairs={{0,8},{4,12},{8,0},{12,4},{16,24},{20,28},{24,16},{28,20},{1,9},{5... | collective-permute-start | bytes 884744 | tf_op jit(solution)/shard_map/ppermute | solution.py:323
  271.6 14.9 %collective-permute-start.16 = (bf16[2,1,1,1,1,24,3072]{6,5,4,3,2,1,0:T(8,128)(2,1)S(1)}, bf16[2,1,1,1,1,24,3072]{6,5,4,3,2,1,0:T(8,128)(2,1)S(1)}, u32[]{:S(2)}, u32[]{:S(2)}) collective-permute-start(bf16[2,1,1,1,1,24,3072]{6,5,4,3,2,1,0:T(8,128)(2,1)S(1)} %constant_dynamic-slice_fusion.15), channel_id=1, source_target_pairs={{0,8},{4,12},{8,0},{12,4},{16,24},{20,28},{24,16},{28,20},{1,9},{5... | collective-permute-start | bytes 884744 | tf_op jit(solution)/shard_map/ppermute | solution.py:323
  271.7 21.8 %collective-permute-start.17 = (bf16[2,2,1,2,1,24,2304]{6,5,4,3,2,1,0:T(8,128)(2,1)S(1)}, bf16[2,2,1,2,1,24,2304]{6,5,4,3,2,1,0:T(8,128)(2,1)S(1)}, u32[]{:S(2)}, u32[]{:S(2)}) collective-permute-start(bf16[2,2,1,2,1,24,2304]{6,5,4,3,2,1,0:T(8,128)(2,1)S(1)} %constant_dynamic-slice_fusion.14), channel_id=1, source_target_pairs={{0,4},{4,0},{8,12},{12,8},{16,20},{20,16},{24,28},{28,24},{1,5},{5... | collective-permute-start | bytes 2654216 | tf_op jit(solution)/shard_map/ppermute | solution.py:323
  273.6 20.0 %collective-permute-start.18 = (bf16[1,196,768]{2,1,0:T(8,128)(2,1)S(1)}, bf16[1,196,768]{2,1,0:T(8,128)(2,1)S(1)}, u32[]{:S(2)}, u32[]{:S(2)}) collective-permute-start(bf16[1,196,768]{2,1,0:T(8,128)(2,1)S(1)} %get-tuple-element.169), channel_id=1, source_target_pairs={{0,1},{1,0},{2,3},{3,2},{4,5},{5,4},{6,7},{7,6},{8,9},{9,8},{10,11... | collective-permute-start | bytes 903176 | tf_op jit(solution)/shard_map/ppermute | solution.py:349
  273.6 20.0 %collective-permute-start.19 = (bf16[1,196,768]{2,1,0:T(8,128)(2,1)S(1)}, bf16[1,196,768]{2,1,0:T(8,128)(2,1)S(1)}, u32[]{:S(2)}, u32[]{:S(2)}) collective-permute-start(bf16[1,196,768]{2,1,0:T(8,128)(2,1)S(1)} %get-tuple-element.168), channel_id=1, source_target_pairs={{0,2},{1,3},{2,0},{3,1},{4,6},{5,7},{6,4},{7,5},{8,10},{9,11},{10,... | collective-permute-start | bytes 903176 | tf_op jit(solution)/shard_map/ppermute | solution.py:349
  285.1 9.2 %collective-permute-start.20 = (bf16[1,196,768]{2,1,0:T(8,128)(2,1)S(1)}, bf16[1,196,768]{2,1,0:T(8,128)(2,1)S(1)}, u32[]{:S(2)}, u32[]{:S(2)}) collective-permute-start(bf16[1,196,768]{2,1,0:T(8,128)(2,1)S(1)} %get-tuple-element.167), channel_id=1, source_target_pairs={{0,3},{1,2},{2,1},{3,0},{4,7},{5,6},{6,5},{7,4},{8,11},{9,10},{10,... | collective-permute-start | bytes 903176 | tf_op jit(solution)/shard_map/ppermute | solution.py:349
  306.2 20.5 %collective-permute-start.21 = (bf16[2,2,1,1,1,24,2304]{6,5,4,3,2,1,0:T(8,128)(2,1)}, bf16[2,2,1,1,1,24,2304]{6,5,4,3,2,1,0:T(8,128)(2,1)}, u32[]{:S(2)}, u32[]{:S(2)}) collective-permute-start(bf16[2,2,1,1,1,24,2304]{6,5,4,3,2,1,0:T(8,128)(2,1)} %constant_dynamic-slice_fusion.13), channel_id=1, source_target_pairs={{0,2},{1,3},{2,0},{3,1},{4,6},{5,7},{6,4},{7,5},{8,10},{9,11},{10,... | collective-permute-start | bytes 1327112 | tf_op jit(solution)/shard_map/ppermute | solution.py:323
  308.0 17.7 %collective-permute-start.22 = (bf16[1,1,1,1,1,96,768]{6,5,4,3,2,1,0:T(8,128)(2,1)}, bf16[1,1,1,1,1,96,768]{6,5,4,3,2,1,0:T(8,128)(2,1)}, u32[]{:S(2)}, u32[]{:S(2)}) collective-permute-start(bf16[1,1,1,1,1,96,768]{6,5,4,3,2,1,0:T(8,128)(2,1)} %constant_dynamic-slice_fusion.12), channel_id=1, source_target_pairs={{0,16},{4,20},{8,24},{12,28},{16,0},{20,4},{24,8},{28,12},{1,17},{... | collective-permute-start | bytes 442376 | tf_op jit(solution)/shard_map/ppermute | solution.py:323
  311.7 13.1 %collective-permute-start.23 = (bf16[1,1,1,1,1,24,3072]{6,5,4,3,2,1,0:T(8,128)(2,1)}, bf16[1,1,1,1,1,24,3072]{6,5,4,3,2,1,0:T(8,128)(2,1)}, u32[]{:S(2)}, u32[]{:S(2)}) collective-permute-start(bf16[1,1,1,1,1,24,3072]{6,5,4,3,2,1,0:T(8,128)(2,1)} %constant_dynamic-slice_fusion.11), channel_id=1, source_target_pairs={{0,16},{4,20},{8,24},{12,28},{16,0},{20,4},{24,8},{28,12},{1,17},{... | collective-permute-start | bytes 442376 | tf_op jit(solution)/shard_map/ppermute | solution.py:323
  314.8 13.0 %collective-permute-start.24 = (bf16[2,2,2,2,1,24,1920]{6,5,4,3,2,1,0:T(8,128)(2,1)}, bf16[2,2,2,2,1,24,1920]{6,5,4,3,2,1,0:T(8,128)(2,1)}, u32[]{:S(2)}, u32[]{:S(2)}) collective-permute-start(bf16[2,2,2,2,1,24,1920]{6,5,4,3,2,1,0:T(8,128)(2,1)} %constant_dynamic-slice_fusion.10), channel_id=1, source_target_pairs={{0,1},{1,0},{2,3},{3,2},{4,5},{5,4},{6,7},{7,6},{8,9},{9,8},{10,11... | collective-permute-start | bytes 4423688 | tf_op jit(solution)/shard_map/ppermute | solution.py:323
  318.9 10.5 %collective-permute-start.25 = (bf16[2,2,2,2,1,24,2048]{6,5,4,3,2,1,0:T(8,128)(2,1)S(1)}, bf16[2,2,2,2,1,24,2048]{6,5,4,3,2,1,0:T(8,128)(2,1)S(1)}, u32[]{:S(2)}, u32[]{:S(2)}) collective-permute-start(bf16[2,2,2,2,1,24,2048]{6,5,4,3,2,1,0:T(8,128)(2,1)S(1)} %fusion.16), channel_id=1, source_target_pairs={{0,1},{1,0},{2,3},{3,2},{4,5},{5,4},{6,7},{7,6},{8,9},{9,8},{10,11... | collective-permute-start | bytes 4718600 | tf_op jit(solution)/shard_map/ppermute | solution.py:323
  334.5 16.9 %collective-permute-start.29 = (bf16[2,2,1,2,1,24,1920]{6,5,4,3,2,1,0:T(8,128)(2,1)S(1)}, bf16[2,2,1,2,1,24,1920]{6,5,4,3,2,1,0:T(8,128)(2,1)S(1)}, u32[]{:S(2)}, u32[]{:S(2)}) collective-permute-start(bf16[2,2,1,2,1,24,1920]{6,5,4,3,2,1,0:T(8,128)(2,1)S(1)} %constant_dynamic-slice_fusion.6), channel_id=1, source_target_pairs={{0,4},{4,0},{8,12},{12,8},{16,20},{20,16},{24,28},{28,24},{1,5},{5... | collective-permute-start | bytes 2211848 | tf_op jit(solution)/shard_map/ppermute | solution.py:323
  335.6 17.7 %collective-permute-start.30 = (bf16[2,2,2,1,1,24,2048]{6,5,4,3,2,1,0:T(8,128)(2,1)S(1)}, bf16[2,2,2,1,1,24,2048]{6,5,4,3,2,1,0:T(8,128)(2,1)S(1)}, u32[]{:S(2)}, u32[]{:S(2)}) collective-permute-start(bf16[2,2,2,1,1,24,2048]{6,5,4,3,2,1,0:T(8,128)(2,1)S(1)} %constant_dynamic-slice_fusion.5), channel_id=1, source_target_pairs={{0,2},{1,3},{2,0},{3,1},{4,6},{5,7},{6,4},{7,5},{8,10},{9,11},{10,... | collective-permute-start | bytes 2359304 | tf_op jit(solution)/shard_map/ppermute | solution.py:323
  363.7 11.5 %collective-permute-start.35 = (bf16[1,1,1,1,1,24,3968]{6,5,4,3,2,1,0:T(8,128)(2,1)S(1)}, bf16[1,1,1,1,1,24,3968]{6,5,4,3,2,1,0:T(8,128)(2,1)S(1)}, u32[]{:S(2)}, u32[]{:S(2)}) collective-permute-start(bf16[1,1,1,1,1,24,3968]{6,5,4,3,2,1,0:T(8,128)(2,1)S(1)} %get-tuple-element.178), channel_id=1, source_target_pairs={{0,24},{4,28},{8,16},{12,20},{16,8},{20,12},{24,0},{28,4},{1,25},{... | collective-permute-start | bytes 571400 | tf_op jit(solution)/shard_map/ppermute | solution.py:323
  365.6 9.7 %collective-permute-start.34 = (bf16[1,1,1,1,1,24,3968]{6,5,4,3,2,1,0:T(8,128)(2,1)S(1)}, bf16[1,1,1,1,1,24,3968]{6,5,4,3,2,1,0:T(8,128)(2,1)S(1)}, u32[]{:S(2)}, u32[]{:S(2)}) collective-permute-start(bf16[1,1,1,1,1,24,3968]{6,5,4,3,2,1,0:T(8,128)(2,1)S(1)} %get-tuple-element.179), channel_id=1, source_target_pairs={{0,8},{4,12},{8,0},{12,4},{16,24},{20,28},{24,16},{28,20},{1,9},{5... | collective-permute-start | bytes 571400 | tf_op jit(solution)/shard_map/ppermute | solution.py:323
  365.6 13.6 %collective-permute-start.33 = (bf16[1,1,1,1,1,24,3968]{6,5,4,3,2,1,0:T(8,128)(2,1)S(1)}, bf16[1,1,1,1,1,24,3968]{6,5,4,3,2,1,0:T(8,128)(2,1)S(1)}, u32[]{:S(2)}, u32[]{:S(2)}) collective-permute-start(bf16[1,1,1,1,1,24,3968]{6,5,4,3,2,1,0:T(8,128)(2,1)S(1)} %get-tuple-element.177), channel_id=1, source_target_pairs={{0,16},{4,20},{8,24},{12,28},{16,0},{20,4},{24,8},{28,12},{1,17},{... | collective-permute-start | bytes 571400 | tf_op jit(solution)/shard_map/ppermute | solution.py:323
  (73 other events, 843.6 us)
Sparse Core Ops, SparseCore 0:
  11.5 124.8 all-gather.1
where the time goes:
time: 397 us; the launch traced here: 389 us
  waiting for transfers between devices  117 us (29%)
  local copies, waits for them, and re-layouts  65.6 us (17%)
  Pallas kernels  60.3 us (15%)
  starting transfers between devices  43.6 us (11%)
  matrix products  43.5 us (11%)
  other arithmetic  35.8 us (9%)
  between operations  23.4 us (6%)
    ppermute x25, waiting for transfers between devices, step(): total = total + lax.ppermute(self.part(places, turn), axis, pairs)  46 us
    ppermute x5, waiting for transfers between devices, step(): other = lax.ppermute(self.piece, place[0], swap_pairs(*place))  35.2 us
    ppermute x25, starting transfers between devices, step(): total = total + lax.ppermute(self.part(places, turn), axis, pairs)  32.5 us
    all_gather x1, waiting for transfers between devices, shards(): lax.all_gather(lay_side_by_side(reduce_blocks + [expand_weight, cross_pai...  30.4 us
    pallas_call x4, Pallas kernels, attention(): pl.pallas_call(body, grid_spec=pltpu.PrefetchScalarGridSpec(num_scalar_pr...  29.1 us
    pallas_call x1, Pallas kernels, ffn(): pl.pallas_call(functools.partial(ffn_body, ratio=ratio), grid=(hidden_wid...  25.7 us
    unnamed x145, local copies, waits for them, and re-layouts  18.4 us
    add x20, other arithmetic, step(): total = total + lax.ppermute(self.part(places, turn), axis, pairs)  16.6 us
  transfers between devices with their start and end apart: 37, of which 18 were waited for; matrix products, arithmetic and copies ran while one was open for 24% of the time, Pallas kernels for 7%

commit v1 on v0

--- a/solution.py
+++ b/solution.py
@@ -433,25 +433,27 @@
     reduce_blocks = [reduce_weight[k * rows : (k + 1) * rows] for k in range(ratio)]
     wide = lax.all_gather(
         lay_side_by_side(
-            reduce_blocks + [expand_weight, cross_pair, self_output, cross_query, cross_output]
+            reduce_blocks + [expand_weight, cross_pair, cross_query, cross_output]
         ),
         ("dp", "seq"),
         axis=0,
         tiled=True,
     )
-    first_group = Gather(jnp.concatenate([self_packed, norm_columns], axis=1), False)
+    first_group = Gather(
+        jnp.concatenate([self_packed, self_output, norm_columns], axis=1), False
+    )
     while first_group.left:
         first_group.step()
     first_group = first_group.rows()
     packed_weight = first_group[:, : 3 * model_width]
-    norm_values = first_group[:, 3 * model_width : 3 * model_width + 6].astype(jnp.float32)
+    output_weight = first_group[:, 3 * model_width : 4 * model_width]
+    norm_values = first_group[:, 4 * model_width : 4 * model_width + 6].astype(jnp.float32)
     norm_gains, norm_shifts = norm_values[:, :3], norm_values[:, 3:]
     hidden_width = expand_weight.shape[1]
     narrower = wide[:, 2 * hidden_width :]
     pair_weight = narrower[:, : 2 * model_width]
-    output_weight = narrower[:, 2 * model_width : 3 * model_width]
-    query_weight = narrower[:, 3 * model_width : 4 * model_width]
-    cross_weight = narrower[:, 4 * model_width :]
+    query_weight = narrower[:, 2 * model_width : 3 * model_width]
+    cross_weight = narrower[:, 3 * model_width :]
 
     live_rows = jnp.arange(seq_len)[None, :] < caption_lengths[:, None]
     inputs = caption_tokens.astype(jnp.float32)
@@ -504,10 +506,10 @@
     cross_sums = Scatter(
         narrow(jnp.concatenate([cross_pair_grad, cross_output_grad], axis=1)), True, 2
     )
-    grad_pair, grad_cross_rows = advance(
-        [reduce_sums, expand_sums, cross_sums], grad_pair, grad_cross_rows
-    )
     image_rows = project_back(grad_pair, pair_weight).astype(jnp.bfloat16)
+    image_rows, grad_cross_rows = advance(
+        [reduce_sums, expand_sums, cross_sums], image_rows, grad_cross_rows
+    )
     cross_query_grad = weight_grad(normed_two, grad_cross_rows)
     grad_norm_two, gain_two, shift_two = norm_back(
         project_back(grad_cross_rows, query_weight).astype(jnp.bfloat16).astype(jnp.float32),

time: 397 us -> 401 us (1.010)
  waiting for transfers between devices: 117 us -> 127 us
  starting transfers between devices: 43.6 us -> 38.3 us
    ppermute x5, waiting for transfers between devices: 35.2 us -> 71.5 us  [step(): other = lax.ppermute(self.piece, place[0], swap_pairs(*place))]
    all_gather x1, waiting for transfers between devices: 30.4 us -> 0.02 us  [shards(): lax.all_gather(lay_side_by_side(reduce_blocks + [expand_weight, cross_pai...]
    ppermute x6, waiting for transfers between devices: 5.48 us -> 12.7 us  [swap(): lax.ppermute(rows, 'seq', [(i, i ^ k) for i in range(lax.axis_size('seq'))])]
    ppermute x25, starting transfers between devices: 32.5 us -> 27.7 us  [step(): total = total + lax.ppermute(self.part(places, turn), axis, pairs)]
    unnamed x145 -> x149, local copies, waits for them, and re-layouts: 18.4 us -> 16.8 us
  transfers between devices with their start and end apart: 37 -> 37, of which waited for: 18 -> 18; matrix products, arithmetic and copies ran while one was open for 24% -> 25% of each run, Pallas kernels for 7% -> 7%
where the time goes in v1:
time: 401 us; the launch traced here: 393 us
  waiting for transfers between devices  127 us (32%)
  local copies, waits for them, and re-layouts  64.1 us (16%)
  Pallas kernels  60.3 us (15%)
  matrix products  44 us (11%)
  starting transfers between devices  38.3 us (10%)
  other arithmetic  35.8 us (9%)
  between operations  23.4 us (6%)
    ppermute x5, waiting for transfers between devices, step(): other = lax.ppermute(self.piece, place[0], swap_pairs(*place))  71.5 us
    ppermute x25, waiting for transfers between devices, step(): total = total + lax.ppermute(self.part(places, turn), axis, pairs)  42.6 us
    pallas_call x4, Pallas kernels, attention(): pl.pallas_call(body, grid_spec=pltpu.PrefetchScalarGridSpec(num_scalar_pr...  29.1 us
    ppermute x25, starting transfers between devices, step(): total = total + lax.ppermute(self.part(places, turn), axis, pairs)  27.7 us
    pallas_call x1, Pallas kernels, ffn(): pl.pallas_call(functools.partial(ffn_body, ratio=ratio), grid=(hidden_wid...  25.7 us
    dot_general x5, matrix products, project_back(): lax.dot_general(flat_rows, weight, (((1,), (1,)), ((), ())), preferred_el...  17.4 us
    unnamed x149, local copies, waits for them, and re-layouts  16.8 us
    add x20, other arithmetic, step(): total = total + lax.ppermute(self.part(places, turn), axis, pairs)  16.5 us
  transfers between devices with their start and end apart: 37, of which 18 were waited for; matrix products, arithmetic and copies ran while one was open for 25% of the time, Pallas kernels for 7%

profile of v1, /device:TPU:0, one launch (start us, length us, event | category | flops | bytes accessed | tf_op | source)
XLA Modules:
  0.0 392.9 jit_solution(5588828332711810943)
XLA Ops:
  10.8 4.1 %collective-permute-start = (bf16[1,1,1,1,1,24,3200]{6,5,4,3,2,1,0:T(8,128)(2,1)S(1)}, bf16[1,1,1,1,1,24,3200]{6,5,4,3,2,1,0:T(8,128)(2,1)S(1)}, u32[]{:S(2)}, u32[]{:S(2)}) collective-permute-start(bf16[1,1,1,1,1,24,3200]{6,5,4,3,2,1,0:T(8,128)(2,1)S(1)} %fusion.25), channel_id=1, source_target_pairs={{0,16},{4,20},{8,24},{12,28},{16,0},{20,4},{24,8},{28,12},{1,17},{... | collective-permute-start | bytes 460808 | tf_op jit(solution)/shard_map/ppermute | solution.py:288
  18.1 4.1 %collective-permute-done = bf16[1,1,1,1,1,24,3200]{6,5,4,3,2,1,0:T(8,128)(2,1)S(1)} collective-permute-done((bf16[1,1,1,1,1,24,3200]{6,5,4,3,2,1,0:T(8,128)(2,1)S(1)}, bf16[1,1,1,1,1,24,3200]{6,5,4,3,2,1,0:T(8,128)(2,1)S(1)}, u32[]{:S(2)}, u32[]{:S(2)}) %collective-permute-start) | collective-permute-done | bytes 153632 | tf_op jit(solution)/shard_map/ppermute | solution.py:288
  24.7 16.8 %collective-permute-done.1 = bf16[2,1,1,1,1,24,3200]{6,5,4,3,2,1,0:T(8,128)(2,1)S(1)} collective-permute-done((bf16[2,1,1,1,1,24,3200]{6,5,4,3,2,1,0:T(8,128)(2,1)S(1)}, bf16[2,1,1,1,1,24,3200]{6,5,4,3,2,1,0:T(8,128)(2,1)S(1)}, u32[]{:S(2)}, u32[]{:S(2)}) %collective-permute-start.1) | collective-permute-done | bytes 307232 | tf_op jit(solution)/shard_map/ppermute | solution.py:288
  44.5 24.1 %collective-permute-done.2 = bf16[2,2,1,1,1,24,3200]{6,5,4,3,2,1,0:T(8,128)(2,1)S(1)} collective-permute-done((bf16[2,2,1,1,1,24,3200]{6,5,4,3,2,1,0:T(8,128)(2,1)S(1)}, bf16[2,2,1,1,1,24,3200]{6,5,4,3,2,1,0:T(8,128)(2,1)S(1)}, u32[]{:S(2)}, u32[]{:S(2)}) %collective-permute-start.2) | collective-permute-done | bytes 614432 | tf_op jit(solution)/shard_map/ppermute | solution.py:288
  80.9 26.6 %collective-permute-done.3 = bf16[2,2,2,1,1,24,3200]{6,5,4,3,2,1,0:T(8,128)(2,1)S(1)} collective-permute-done((bf16[2,2,2,1,1,24,3200]{6,5,4,3,2,1,0:T(8,128)(2,1)S(1)}, bf16[2,2,2,1,1,24,3200]{6,5,4,3,2,1,0:T(8,128)(2,1)S(1)}, u32[]{:S(2)}, u32[]{:S(2)}) %collective-permute-start.3) | collective-permute-done | bytes 1228832 | tf_op jit(solution)/shard_map/ppermute | solution.py:288
  108.6 3.4 constant_dynamic-slice_fusion.28
  121.0 6.0 %collective-permute-done.6 = bf16[1,196,768]{2,1,0:T(8,128)(2,1)S(1)} collective-permute-done((bf16[1,196,768]{2,1,0:T(8,128)(2,1)S(1)}, bf16[1,196,768]{2,1,0:T(8,128)(2,1)S(1)}, u32[]{:S(2)}, u32[]{:S(2)}) %collective-permute-start.6) | collective-permute-done | bytes 301088 | tf_op jit(solution)/shard_map/ppermute | solution.py:349
  127.8 5.3 %collective-permute-done.7 = bf16[1,196,768]{2,1,0:T(8,128)(2,1)S(1)} collective-permute-done((bf16[1,196,768]{2,1,0:T(8,128)(2,1)S(1)}, bf16[1,196,768]{2,1,0:T(8,128)(2,1)S(1)}, u32[]{:S(2)}, u32[]{:S(2)}) %collective-permute-start.7) | collective-permute-done | bytes 301088 | tf_op jit(solution)/shard_map/ppermute | solution.py:349
  133.8 3.5 constant_dynamic-update-slice_fusion
  139.5 4.4 %convolution_convert_fusion.query_ref.key_ref.value_ref.refs_1_.refs_2_.refs_3_ = bf16[4,128,2304]{2,1,0:T(8,128)(2,1)S(1)} fusion(bf16[768,3200]{1,0:T(8,128)(2,1)} %bitcast.1, f32[768]{0:T(1024)S(1)} %get-tuple-element.159, f32[768]{0:T(1024)S(1)} %get-tuple-element.160, f32[4,128]{1,0:T(4,128)S(1)} %add_rsqrt_fusion.2, ...), kind=kOutput, calls=%fused_computation.2 | convolution fusion | flops 1815478272 | bytes 6694912 | tf_op jit(solution)/shard_map/dot_general | solution.py:25
  143.9 4.5 %self_attention.1 = bf16[4,128,768]{2,1,0:T(8,128)(2,1)S(1)} custom-call(s32[4]{0:T(128)S(1)} %copy-done.10, bf16[4,128,2304]{2,1,0:T(8,128)(2,1)S(1)} %convolution_convert_fusion.query_ref.key_ref.value_ref.refs_1_.refs_2_.refs_3_, bf16[4,128,2304]{2,1,0:T(8,128)(2,1)S(1)} %convolution_convert_fusion.query_ref.key_ref.value_ref.refs_1_.refs_2_.refs_3_, ...), custom_call_target="tpu_custom_call" | custom-call | flops 201326592 | tf_op jit(solution)/shard_map/self_attention/pallas_call | solution.py:198
  152.4 4.2 %convolution_convert_fusion.1.key_ref.value_ref = bf16[4,196,1536]{2,1,0:T(8,128)(2,1)S(1)} fusion(bf16[4,196,768]{2,1,0:T(8,128)(2,1)} %constant_dynamic-update-slice_fusion.6, bf16[768,9216]{1,0:T(8,128)(2,1)} %all-gather.2.cloned.1.call-done.expand_ref.reduce_ref), kind=kOutput, calls=%fused_computation.7 | convolution fusion | flops 1850892288 | bytes 5996544 | tf_op jit(solution)/shard_map/dot_general | solution.py:25
  156.6 3.1 convolution_convert_fusion.6.query_ref
  159.7 4.1 %cross_attention.1 = bf16[4,128,768]{2,1,0:T(8,128)(2,1)S(1)} custom-call(s32[4]{0:T(128)S(1)} %broadcast_xor_fusion.table_ref, bf16[4,128,768]{2,1,0:T(8,128)(2,1)S(1)} %convolution_convert_fusion.6.query_ref, bf16[4,196,1536]{2,1,0:T(8,128)(2,1)S(1)} %convolution_convert_fusion.1.key_ref.value_ref, ...), custom_call_target="tpu_custom_call" | custom-call | flops 308281344 | tf_op jit(solution)/shard_map/cross_attention/pallas_call | solution.py:198
  168.0 25.7 %ffn.1 = (f32[512,768]{1,0:T(8,128)S(1)}, f32[512,768]{1,0:T(8,128)S(1)}, bf16[3072,768]{1,0:T(8,128)(2,1)}, bf16[768,3072]{1,0:T(8,128)(2,1)}) custom-call(bf16[512,768]{1,0:T(8,128)(2,1)S(1)} %bitcast.110, bf16[512,768]{1,0:T(8,128)(2,1)S(1)} %bitcast.109, bf16[768,9216]{1,0:T(8,128)(2,1)} %all-gather.2.cloned.1.call-done.expand_ref.reduce_ref, ...), custom_call_target="tpu_custom_call" | custom-call | tf_op jit(solution)/shard_map/ffn/pallas_call | solution.py:103
  193.7 4.4 %constant_dynamic-slice_fusion.23 = bf16[2,2,2,2,1,96,768]{6,5,4,3,2,1,0:T(8,128)(2,1)} fusion(bf16[2,2,2,2,2,96,768]{6,5,4,3,2,1,0:T(8,128)(2,1)} %bitcast.120, s32[]{:T(128)S(6)} %select_n.225), kind=kLoop, calls=%fused_computation.128 | loop fusion | bytes 4718596 | tf_op jit(solution)/shard_map/dynamic_slice | solution.py:313
  205.7 2.9 convolution_convert_fusion.4.grad_ref
  217.8 11.8 %cross_backward.1 = (bf16[4,128,768]{2,1,0:T(8,128)(2,1)S(1)}, bf16[4,196,1536]{2,1,0:T(8,128)(2,1)S(1)}) custom-call(s32[4]{0:T(128)S(1)} %broadcast_xor_fusion.table_ref, bf16[4,128,768]{2,1,0:T(8,128)(2,1)S(1)} %copy-done.4, bf16[4,196,1536]{2,1,0:T(8,128)(2,1)} %copy-done, bf16[4,196,1536]{2,1,0:T(8,128)(2,1)} %copy-done, ...), custom_call_target="tpu_custom_call" | custom-call | flops 770703360 | tf_op jit(solution)/shard_map/cross_backward/pallas_call | solution.py:198
  229.7 2.9 bitcast_convert_fusion.1
  233.7 6.1 %fusion.21 = bf16[4,196,768]{2,1,0:T(8,128)(2,1)} fusion(bf16[4,196,1536]{2,1,0:T(8,128)(2,1)S(1)} %get-tuple-element.62, bf16[768,9216]{1,0:T(8,128)(2,1)} %all-gather.2.cloned.1.call-done.expand_ref.reduce_ref), kind=kOutput, calls=%fused_computation.58 | convolution fusion | flops 1850290176 | bytes 5971968 | tf_op jit(solution)/shard_map/dot_general | solution.py:32
  239.8 3.4 collective-permute-done.10
  275.4 8.7 %self_backward.1 = bf16[4,128,2304]{2,1,0:T(8,128)(2,1)S(1)} custom-call(s32[4]{0:T(128)S(1)} %copy-done.10, bf16[4,128,2304]{2,1,0:T(8,128)(2,1)S(1)} %convolution_convert_fusion.query_ref.key_ref.value_ref.refs_1_.refs_2_.refs_3_, bf16[4,128,2304]{2,1,0:T(8,128)(2,1)S(1)} %convolution_convert_fusion.query_ref.key_ref.value_ref.refs_1_.refs_2_.refs_3_, ...), custom_call_target="tpu_custom_call" | custom-call | flops 503316480 | tf_op jit(solution)/shard_map/self_backward/pallas_call | solution.py:198
  285.1 6.7 %collective-permute-done.17 = bf16[2,2,1,2,1,24,2304]{6,5,4,3,2,1,0:T(8,128)(2,1)S(1)} collective-permute-done((bf16[2,2,1,2,1,24,2304]{6,5,4,3,2,1,0:T(8,128)(2,1)S(1)}, bf16[2,2,1,2,1,24,2304]{6,5,4,3,2,1,0:T(8,128)(2,1)S(1)}, u32[]{:S(2)}, u32[]{:S(2)}) %collective-permute-start.17) | collective-permute-done | bytes 884768 | tf_op jit(solution)/shard_map/ppermute | solution.py:323
  297.4 4.0 %fusion.1 = f32[512,768]{1,0:T(8,128)S(1)} fusion(bf16[512,2304]{1,0:T(8,128)(2,1)S(1)} %bitcast.111, bf16[768,3200]{1,0:T(8,128)(2,1)} %bitcast.1), kind=kOutput, calls=%fused_computation.8 | convolution fusion | flops 1811939328 | bytes 7471104 | tf_op jit(solution)/shard_map/dot_general | solution.py:32
  305.9 5.6 %collective-permute-start.22 = (bf16[1,1,1,1,1,96,768]{6,5,4,3,2,1,0:T(8,128)(2,1)}, bf16[1,1,1,1,1,96,768]{6,5,4,3,2,1,0:T(8,128)(2,1)}, u32[]{:S(2)}, u32[]{:S(2)}) collective-permute-start(bf16[1,1,1,1,1,96,768]{6,5,4,3,2,1,0:T(8,128)(2,1)} %constant_dynamic-slice_fusion.12), channel_id=1, source_target_pairs={{0,16},{4,20},{8,24},{12,28},{16,0},{20,4},{24,8},{28,12},{1,17},{... | collective-permute-start | bytes 442376 | tf_op jit(solution)/shard_map/ppermute | solution.py:323
  330.5 3.6 collective-permute-start.28
  338.3 3.1 collective-permute-done.27
  342.8 9.9 %collective-permute-done.29 = bf16[2,2,1,2,1,24,1920]{6,5,4,3,2,1,0:T(8,128)(2,1)S(1)} collective-permute-done((bf16[2,2,1,2,1,24,1920]{6,5,4,3,2,1,0:T(8,128)(2,1)S(1)}, bf16[2,2,1,2,1,24,1920]{6,5,4,3,2,1,0:T(8,128)(2,1)S(1)}, u32[]{:S(2)}, u32[]{:S(2)}) %collective-permute-start.29) | collective-permute-done | bytes 737312 | tf_op jit(solution)/shard_map/ppermute | solution.py:323
  358.8 6.6 %collective-permute-done.31 = bf16[2,2,1,1,1,24,1920]{6,5,4,3,2,1,0:T(8,128)(2,1)S(1)} collective-permute-done((bf16[2,2,1,1,1,24,1920]{6,5,4,3,2,1,0:T(8,128)(2,1)S(1)}, bf16[2,2,1,1,1,24,1920]{6,5,4,3,2,1,0:T(8,128)(2,1)S(1)}, u32[]{:S(2)}, u32[]{:S(2)}) %collective-permute-start.31) | collective-permute-done | bytes 368672 | tf_op jit(solution)/shard_map/ppermute | solution.py:323
  365.7 3.5 collective-permute-start.35
  370.9 3.6 put_rows.1
  377.2 5.6 %collective-permute-done.33 = bf16[1,1,1,1,1,24,3968]{6,5,4,3,2,1,0:T(8,128)(2,1)S(1)} collective-permute-done((bf16[1,1,1,1,1,24,3968]{6,5,4,3,2,1,0:T(8,128)(2,1)S(1)}, bf16[1,1,1,1,1,24,3968]{6,5,4,3,2,1,0:T(8,128)(2,1)S(1)}, u32[]{:S(2)}, u32[]{:S(2)}) %collective-permute-start.33) | collective-permute-done | bytes 190496 | tf_op jit(solution)/shard_map/ppermute | solution.py:323
  (336 shorter events, 137.3 us)
Async XLA Ops:
  7.2 145.2 %all-gather.2.cloned.1.call-start = ((), (), s32[]{:S(2)}) async-start(), calls=%async_computation | async-start | bytes 14598144 | tf_op jit(solution)/shard_map/all_gather | solution.py:434
  10.8 11.4 %collective-permute-start = (bf16[1,1,1,1,1,24,3200]{6,5,4,3,2,1,0:T(8,128)(2,1)S(1)}, bf16[1,1,1,1,1,24,3200]{6,5,4,3,2,1,0:T(8,128)(2,1)S(1)}, u32[]{:S(2)}, u32[]{:S(2)}) collective-permute-start(bf16[1,1,1,1,1,24,3200]{6,5,4,3,2,1,0:T(8,128)(2,1)S(1)} %fusion.25), channel_id=1, source_target_pairs={{0,16},{4,20},{8,24},{12,28},{16,0},{20,4},{24,8},{28,12},{1,17},{... | collective-permute-start | bytes 460808 | tf_op jit(solution)/shard_map/ppermute | solution.py:288
  23.9 17.6 %collective-permute-start.1 = (bf16[2,1,1,1,1,24,3200]{6,5,4,3,2,1,0:T(8,128)(2,1)S(1)}, bf16[2,1,1,1,1,24,3200]{6,5,4,3,2,1,0:T(8,128)(2,1)S(1)}, u32[]{:S(2)}, u32[]{:S(2)}) collective-permute-start(bf16[2,1,1,1,1,24,3200]{6,5,4,3,2,1,0:T(8,128)(2,1)S(1)} %constant_dynamic-slice_fusion.31), channel_id=1, source_target_pairs={{0,8},{4,12},{8,0},{12,4},{16,24},{20,28},{24,16},{28,20},{1,9},{5... | collective-permute-start | bytes 921608 | tf_op jit(solution)/shard_map/ppermute | solution.py:288
  43.3 25.3 %collective-permute-start.2 = (bf16[2,2,1,1,1,24,3200]{6,5,4,3,2,1,0:T(8,128)(2,1)S(1)}, bf16[2,2,1,1,1,24,3200]{6,5,4,3,2,1,0:T(8,128)(2,1)S(1)}, u32[]{:S(2)}, u32[]{:S(2)}) collective-permute-start(bf16[2,2,1,1,1,24,3200]{6,5,4,3,2,1,0:T(8,128)(2,1)S(1)} %constant_dynamic-slice_fusion.30), channel_id=1, source_target_pairs={{0,4},{4,0},{8,12},{12,8},{16,20},{20,16},{24,28},{28,24},{1,5},{5... | collective-permute-start | bytes 1843208 | tf_op jit(solution)/shard_map/ppermute | solution.py:288
  70.9 36.5 %collective-permute-start.3 = (bf16[2,2,2,1,1,24,3200]{6,5,4,3,2,1,0:T(8,128)(2,1)S(1)}, bf16[2,2,2,1,1,24,3200]{6,5,4,3,2,1,0:T(8,128)(2,1)S(1)}, u32[]{:S(2)}, u32[]{:S(2)}) collective-permute-start(bf16[2,2,2,1,1,24,3200]{6,5,4,3,2,1,0:T(8,128)(2,1)S(1)} %constant_dynamic-slice_fusion.29), channel_id=1, source_target_pairs={{0,2},{1,3},{2,0},{3,1},{4,6},{5,7},{6,4},{7,5},{8,10},{9,11},{10,... | collective-permute-start | bytes 3686408 | tf_op jit(solution)/shard_map/ppermute | solution.py:288
  111.9 21.8 %collective-permute-start.4 = (bf16[2,2,2,2,1,24,3200]{6,5,4,3,2,1,0:T(8,128)(2,1)}, bf16[2,2,2,2,1,24,3200]{6,5,4,3,2,1,0:T(8,128)(2,1)}, u32[]{:S(2)}, u32[]{:S(2)}) collective-permute-start(bf16[2,2,2,2,1,24,3200]{6,5,4,3,2,1,0:T(8,128)(2,1)} %constant_dynamic-slice_fusion.28), channel_id=1, source_target_pairs={{0,1},{1,0},{2,3},{3,2},{4,5},{5,4},{6,7},{7,6},{8,9},{9,8},{10,11... | collective-permute-start | bytes 7372808 | tf_op jit(solution)/shard_map/ppermute | solution.py:288
  115.1 11.9 %collective-permute-start.6 = (bf16[1,196,768]{2,1,0:T(8,128)(2,1)S(1)}, bf16[1,196,768]{2,1,0:T(8,128)(2,1)S(1)}, u32[]{:S(2)}, u32[]{:S(2)}) collective-permute-start(bf16[1,196,768]{2,1,0:T(8,128)(2,1)S(1)} %copy.86), channel_id=1, source_target_pairs={{0,2},{1,3},{2,0},{3,1},{4,6},{5,7},{6,4},{7,5},{8,10},{9,11},{10,... | collective-permute-start | bytes 903176 | tf_op jit(solution)/shard_map/ppermute | solution.py:349
  115.7 17.3 %collective-permute-start.7 = (bf16[1,196,768]{2,1,0:T(8,128)(2,1)S(1)}, bf16[1,196,768]{2,1,0:T(8,128)(2,1)S(1)}, u32[]{:S(2)}, u32[]{:S(2)}) collective-permute-start(bf16[1,196,768]{2,1,0:T(8,128)(2,1)S(1)} %copy.87), channel_id=1, source_target_pairs={{0,3},{1,2},{2,1},{3,0},{4,7},{5,6},{6,5},{7,4},{8,11},{9,10},{10,... | collective-permute-start | bytes 903176 | tf_op jit(solution)/shard_map/ppermute | solution.py:349
  198.1 11.6 %collective-permute-start.8 = (bf16[2,2,2,2,1,96,768]{6,5,4,3,2,1,0:T(8,128)(2,1)}, bf16[2,2,2,2,1,96,768]{6,5,4,3,2,1,0:T(8,128)(2,1)}, u32[]{:S(2)}, u32[]{:S(2)}) collective-permute-start(bf16[2,2,2,2,1,96,768]{6,5,4,3,2,1,0:T(8,128)(2,1)} %constant_dynamic-slice_fusion.23), channel_id=1, source_target_pairs={{0,1},{1,0},{2,3},{3,2},{4,5},{5,4},{6,7},{7,6},{8,9},{9,8},{10,11... | collective-permute-start | bytes 7077896 | tf_op jit(solution)/shard_map/ppermute | solution.py:323
  200.0 11.6 %collective-permute-start.9 = (bf16[2,2,2,2,1,24,3072]{6,5,4,3,2,1,0:T(8,128)(2,1)}, bf16[2,2,2,2,1,24,3072]{6,5,4,3,2,1,0:T(8,128)(2,1)}, u32[]{:S(2)}, u32[]{:S(2)}) collective-permute-start(bf16[2,2,2,2,1,24,3072]{6,5,4,3,2,1,0:T(8,128)(2,1)} %constant_dynamic-slice_fusion.22), channel_id=1, source_target_pairs={{0,1},{1,0},{2,3},{3,2},{4,5},{5,4},{6,7},{7,6},{8,9},{9,8},{10,11... | collective-permute-start | bytes 7077896 | tf_op jit(solution)/shard_map/ppermute | solution.py:323
  214.8 28.3 %collective-permute-start.10 = (bf16[2,2,1,2,1,96,768]{6,5,4,3,2,1,0:T(8,128)(2,1)}, bf16[2,2,1,2,1,96,768]{6,5,4,3,2,1,0:T(8,128)(2,1)}, u32[]{:S(2)}, u32[]{:S(2)}) collective-permute-start(bf16[2,2,1,2,1,96,768]{6,5,4,3,2,1,0:T(8,128)(2,1)} %constant_dynamic-slice_fusion.21), channel_id=1, source_target_pairs={{0,4},{4,0},{8,12},{12,8},{16,20},{20,16},{24,28},{28,24},{1,5},{5... | collective-permute-start | bytes 3538952 | tf_op jit(solution)/shard_map/ppermute | solution.py:323
  216.7 28.2 %collective-permute-start.11 = (bf16[2,2,2,1,1,24,3072]{6,5,4,3,2,1,0:T(8,128)(2,1)}, bf16[2,2,2,1,1,24,3072]{6,5,4,3,2,1,0:T(8,128)(2,1)}, u32[]{:S(2)}, u32[]{:S(2)}) collective-permute-start(bf16[2,2,2,1,1,24,3072]{6,5,4,3,2,1,0:T(8,128)(2,1)} %constant_dynamic-slice_fusion.20), channel_id=1, source_target_pairs={{0,2},{1,3},{2,0},{3,1},{4,6},{5,7},{6,4},{7,5},{8,10},{9,11},{10,... | collective-permute-start | bytes 3538952 | tf_op jit(solution)/shard_map/ppermute | solution.py:323
  247.4 16.4 %collective-permute-start.12 = (bf16[2,2,1,1,1,96,768]{6,5,4,3,2,1,0:T(8,128)(2,1)}, bf16[2,2,1,1,1,96,768]{6,5,4,3,2,1,0:T(8,128)(2,1)}, u32[]{:S(2)}, u32[]{:S(2)}) collective-permute-start(bf16[2,2,1,1,1,96,768]{6,5,4,3,2,1,0:T(8,128)(2,1)} %constant_dynamic-slice_fusion.19), channel_id=1, source_target_pairs={{0,2},{1,3},{2,0},{3,1},{4,6},{5,7},{6,4},{7,5},{8,10},{9,11},{10,... | collective-permute-start | bytes 1769480 | tf_op jit(solution)/shard_map/ppermute | solution.py:323
  249.1 16.0 %collective-permute-start.13 = (bf16[2,2,1,1,1,24,3072]{6,5,4,3,2,1,0:T(8,128)(2,1)}, bf16[2,2,1,1,1,24,3072]{6,5,4,3,2,1,0:T(8,128)(2,1)}, u32[]{:S(2)}, u32[]{:S(2)}) collective-permute-start(bf16[2,2,1,1,1,24,3072]{6,5,4,3,2,1,0:T(8,128)(2,1)} %constant_dynamic-slice_fusion.18), channel_id=1, source_target_pairs={{0,4},{4,0},{8,12},{12,8},{16,20},{20,16},{24,28},{28,24},{1,5},{5... | collective-permute-start | bytes 1769480 | tf_op jit(solution)/shard_map/ppermute | solution.py:323
  251.6 14.7 %collective-permute-start.14 = (bf16[2,2,2,2,1,24,2304]{6,5,4,3,2,1,0:T(8,128)(2,1)}, bf16[2,2,2,2,1,24,2304]{6,5,4,3,2,1,0:T(8,128)(2,1)}, u32[]{:S(2)}, u32[]{:S(2)}) collective-permute-start(bf16[2,2,2,2,1,24,2304]{6,5,4,3,2,1,0:T(8,128)(2,1)} %constant_dynamic-slice_fusion.17), channel_id=1, source_target_pairs={{0,1},{1,0},{2,3},{3,2},{4,5},{5,4},{6,7},{7,6},{8,9},{9,8},{10,11... | collective-permute-start | bytes 5308424 | tf_op jit(solution)/shard_map/ppermute | solution.py:323
  268.1 16.1 %collective-permute-start.15 = (bf16[2,1,1,1,1,96,768]{6,5,4,3,2,1,0:T(8,128)(2,1)S(1)}, bf16[2,1,1,1,1,96,768]{6,5,4,3,2,1,0:T(8,128)(2,1)S(1)}, u32[]{:S(2)}, u32[]{:S(2)}) collective-permute-start(bf16[2,1,1,1,1,96,768]{6,5,4,3,2,1,0:T(8,128)(2,1)S(1)} %constant_dynamic-slice_fusion.16), channel_id=1, source_target_pairs={{0,8},{4,12},{8,0},{12,4},{16,24},{20,28},{24,16},{28,20},{1,9},{5... | collective-permute-start | bytes 884744 | tf_op jit(solution)/shard_map/ppermute | solution.py:323
  268.2 16.8 %collective-permute-start.16 = (bf16[2,1,1,1,1,24,3072]{6,5,4,3,2,1,0:T(8,128)(2,1)S(1)}, bf16[2,1,1,1,1,24,3072]{6,5,4,3,2,1,0:T(8,128)(2,1)S(1)}, u32[]{:S(2)}, u32[]{:S(2)}) collective-permute-start(bf16[2,1,1,1,1,24,3072]{6,5,4,3,2,1,0:T(8,128)(2,1)S(1)} %constant_dynamic-slice_fusion.15), channel_id=1, source_target_pairs={{0,8},{4,12},{8,0},{12,4},{16,24},{20,28},{24,16},{28,20},{1,9},{5... | collective-permute-start | bytes 884744 | tf_op jit(solution)/shard_map/ppermute | solution.py:323
  270.3 21.5 %collective-permute-start.17 = (bf16[2,2,1,2,1,24,2304]{6,5,4,3,2,1,0:T(8,128)(2,1)S(1)}, bf16[2,2,1,2,1,24,2304]{6,5,4,3,2,1,0:T(8,128)(2,1)S(1)}, u32[]{:S(2)}, u32[]{:S(2)}) collective-permute-start(bf16[2,2,1,2,1,24,2304]{6,5,4,3,2,1,0:T(8,128)(2,1)S(1)} %constant_dynamic-slice_fusion.14), channel_id=1, source_target_pairs={{0,4},{4,0},{8,12},{12,8},{16,20},{20,16},{24,28},{28,24},{1,5},{5... | collective-permute-start | bytes 2654216 | tf_op jit(solution)/shard_map/ppermute | solution.py:323
  274.3 17.6 %collective-permute-start.18 = (bf16[1,196,768]{2,1,0:T(8,128)(2,1)S(1)}, bf16[1,196,768]{2,1,0:T(8,128)(2,1)S(1)}, u32[]{:S(2)}, u32[]{:S(2)}) collective-permute-start(bf16[1,196,768]{2,1,0:T(8,128)(2,1)S(1)} %get-tuple-element.169), channel_id=1, source_target_pairs={{0,1},{1,0},{2,3},{3,2},{4,5},{5,4},{6,7},{7,6},{8,9},{9,8},{10,11... | collective-permute-start | bytes 903176 | tf_op jit(solution)/shard_map/ppermute | solution.py:349
  274.3 17.6 %collective-permute-start.19 = (bf16[1,196,768]{2,1,0:T(8,128)(2,1)S(1)}, bf16[1,196,768]{2,1,0:T(8,128)(2,1)S(1)}, u32[]{:S(2)}, u32[]{:S(2)}) collective-permute-start(bf16[1,196,768]{2,1,0:T(8,128)(2,1)S(1)} %get-tuple-element.168), channel_id=1, source_target_pairs={{0,2},{1,3},{2,0},{3,1},{4,6},{5,7},{6,4},{7,5},{8,10},{9,11},{10,... | collective-permute-start | bytes 903176 | tf_op jit(solution)/shard_map/ppermute | solution.py:349
  284.2 9.2 %collective-permute-start.20 = (bf16[1,196,768]{2,1,0:T(8,128)(2,1)S(1)}, bf16[1,196,768]{2,1,0:T(8,128)(2,1)S(1)}, u32[]{:S(2)}, u32[]{:S(2)}) collective-permute-start(bf16[1,196,768]{2,1,0:T(8,128)(2,1)S(1)} %get-tuple-element.167), channel_id=1, source_target_pairs={{0,3},{1,2},{2,1},{3,0},{4,7},{5,6},{6,5},{7,4},{8,11},{9,10},{10,... | collective-permute-start | bytes 903176 | tf_op jit(solution)/shard_map/ppermute | solution.py:349
  304.3 22.8 %collective-permute-start.21 = (bf16[2,2,1,1,1,24,2304]{6,5,4,3,2,1,0:T(8,128)(2,1)}, bf16[2,2,1,1,1,24,2304]{6,5,4,3,2,1,0:T(8,128)(2,1)}, u32[]{:S(2)}, u32[]{:S(2)}) collective-permute-start(bf16[2,2,1,1,1,24,2304]{6,5,4,3,2,1,0:T(8,128)(2,1)} %constant_dynamic-slice_fusion.13), channel_id=1, source_target_pairs={{0,2},{1,3},{2,0},{3,1},{4,6},{5,7},{6,4},{7,5},{8,10},{9,11},{10,... | collective-permute-start | bytes 1327112 | tf_op jit(solution)/shard_map/ppermute | solution.py:323
  305.9 20.3 %collective-permute-start.22 = (bf16[1,1,1,1,1,96,768]{6,5,4,3,2,1,0:T(8,128)(2,1)}, bf16[1,1,1,1,1,96,768]{6,5,4,3,2,1,0:T(8,128)(2,1)}, u32[]{:S(2)}, u32[]{:S(2)}) collective-permute-start(bf16[1,1,1,1,1,96,768]{6,5,4,3,2,1,0:T(8,128)(2,1)} %constant_dynamic-slice_fusion.12), channel_id=1, source_target_pairs={{0,16},{4,20},{8,24},{12,28},{16,0},{20,4},{24,8},{28,12},{1,17},{... | collective-permute-start | bytes 442376 | tf_op jit(solution)/shard_map/ppermute | solution.py:323
  312.2 13.1 %collective-permute-start.23 = (bf16[1,1,1,1,1,24,3072]{6,5,4,3,2,1,0:T(8,128)(2,1)}, bf16[1,1,1,1,1,24,3072]{6,5,4,3,2,1,0:T(8,128)(2,1)}, u32[]{:S(2)}, u32[]{:S(2)}) collective-permute-start(bf16[1,1,1,1,1,24,3072]{6,5,4,3,2,1,0:T(8,128)(2,1)} %constant_dynamic-slice_fusion.11), channel_id=1, source_target_pairs={{0,16},{4,20},{8,24},{12,28},{16,0},{20,4},{24,8},{28,12},{1,17},{... | collective-permute-start | bytes 442376 | tf_op jit(solution)/shard_map/ppermute | solution.py:323
  315.3 13.0 %collective-permute-start.24 = (bf16[2,2,2,2,1,24,1920]{6,5,4,3,2,1,0:T(8,128)(2,1)}, bf16[2,2,2,2,1,24,1920]{6,5,4,3,2,1,0:T(8,128)(2,1)}, u32[]{:S(2)}, u32[]{:S(2)}) collective-permute-start(bf16[2,2,2,2,1,24,1920]{6,5,4,3,2,1,0:T(8,128)(2,1)} %constant_dynamic-slice_fusion.10), channel_id=1, source_target_pairs={{0,1},{1,0},{2,3},{3,2},{4,5},{5,4},{6,7},{7,6},{8,9},{9,8},{10,11... | collective-permute-start | bytes 4423688 | tf_op jit(solution)/shard_map/ppermute | solution.py:323
  319.3 10.6 %collective-permute-start.25 = (bf16[2,2,2,2,1,24,2048]{6,5,4,3,2,1,0:T(8,128)(2,1)S(1)}, bf16[2,2,2,2,1,24,2048]{6,5,4,3,2,1,0:T(8,128)(2,1)S(1)}, u32[]{:S(2)}, u32[]{:S(2)}) collective-permute-start(bf16[2,2,2,2,1,24,2048]{6,5,4,3,2,1,0:T(8,128)(2,1)S(1)} %fusion.16), channel_id=1, source_target_pairs={{0,1},{1,0},{2,3},{3,2},{4,5},{5,4},{6,7},{7,6},{8,9},{9,8},{10,11... | collective-permute-start | bytes 4718600 | tf_op jit(solution)/shard_map/ppermute | solution.py:323
  334.1 8.6 %collective-permute-start.26 = (bf16[1,1,1,1,1,24,2304]{6,5,4,3,2,1,0:T(8,128)(2,1)S(1)}, bf16[1,1,1,1,1,24,2304]{6,5,4,3,2,1,0:T(8,128)(2,1)S(1)}, u32[]{:S(2)}, u32[]{:S(2)}) collective-permute-start(bf16[1,1,1,1,1,24,2304]{6,5,4,3,2,1,0:T(8,128)(2,1)S(1)} %get-tuple-element.180), channel_id=1, source_target_pairs={{0,16},{4,20},{8,24},{12,28},{16,0},{20,4},{24,8},{28,12},{1,17},{... | collective-permute-start | bytes 331784 | tf_op jit(solution)/shard_map/ppermute | solution.py:323
  335.0 17.6 %collective-permute-start.29 = (bf16[2,2,1,2,1,24,1920]{6,5,4,3,2,1,0:T(8,128)(2,1)S(1)}, bf16[2,2,1,2,1,24,1920]{6,5,4,3,2,1,0:T(8,128)(2,1)S(1)}, u32[]{:S(2)}, u32[]{:S(2)}) collective-permute-start(bf16[2,2,1,2,1,24,1920]{6,5,4,3,2,1,0:T(8,128)(2,1)S(1)} %constant_dynamic-slice_fusion.6), channel_id=1, source_target_pairs={{0,4},{4,0},{8,12},{12,8},{16,20},{20,16},{24,28},{28,24},{1,5},{5... | collective-permute-start | bytes 2211848 | tf_op jit(solution)/shard_map/ppermute | solution.py:323
  336.1 18.4 %collective-permute-start.30 = (bf16[2,2,2,1,1,24,2048]{6,5,4,3,2,1,0:T(8,128)(2,1)S(1)}, bf16[2,2,2,1,1,24,2048]{6,5,4,3,2,1,0:T(8,128)(2,1)S(1)}, u32[]{:S(2)}, u32[]{:S(2)}) collective-permute-start(bf16[2,2,2,1,1,24,2048]{6,5,4,3,2,1,0:T(8,128)(2,1)S(1)} %constant_dynamic-slice_fusion.5), channel_id=1, source_target_pairs={{0,2},{1,3},{2,0},{3,1},{4,6},{5,7},{6,4},{7,5},{8,10},{9,11},{10,... | collective-permute-start | bytes 2359304 | tf_op jit(solution)/shard_map/ppermute | solution.py:323
  356.0 9.5 %collective-permute-start.32 = (bf16[2,2,1,1,1,24,2048]{6,5,4,3,2,1,0:T(8,128)(2,1)S(1)}, bf16[2,2,1,1,1,24,2048]{6,5,4,3,2,1,0:T(8,128)(2,1)S(1)}, u32[]{:S(2)}, u32[]{:S(2)}) collective-permute-start(bf16[2,2,1,1,1,24,2048]{6,5,4,3,2,1,0:T(8,128)(2,1)S(1)} %constant_dynamic-slice_fusion.3), channel_id=1, source_target_pairs={{0,4},{4,0},{8,12},{12,8},{16,20},{20,16},{24,28},{28,24},{1,5},{5... | collective-permute-start | bytes 1179656 | tf_op jit(solution)/shard_map/ppermute | solution.py:323
  365.7 11.6 %collective-permute-start.35 = (bf16[1,1,1,1,1,24,3968]{6,5,4,3,2,1,0:T(8,128)(2,1)S(1)}, bf16[1,1,1,1,1,24,3968]{6,5,4,3,2,1,0:T(8,128)(2,1)S(1)}, u32[]{:S(2)}, u32[]{:S(2)}) collective-permute-start(bf16[1,1,1,1,1,24,3968]{6,5,4,3,2,1,0:T(8,128)(2,1)S(1)} %get-tuple-element.178), channel_id=1, source_target_pairs={{0,24},{4,28},{8,16},{12,20},{16,8},{20,12},{24,0},{28,4},{1,25},{... | collective-permute-start | bytes 571400 | tf_op jit(solution)/shard_map/ppermute | solution.py:323
  369.1 13.7 %collective-permute-start.33 = (bf16[1,1,1,1,1,24,3968]{6,5,4,3,2,1,0:T(8,128)(2,1)S(1)}, bf16[1,1,1,1,1,24,3968]{6,5,4,3,2,1,0:T(8,128)(2,1)S(1)}, u32[]{:S(2)}, u32[]{:S(2)}) collective-permute-start(bf16[1,1,1,1,1,24,3968]{6,5,4,3,2,1,0:T(8,128)(2,1)S(1)} %get-tuple-element.177), channel_id=1, source_target_pairs={{0,16},{4,20},{8,24},{12,28},{16,0},{20,4},{24,8},{28,12},{1,17},{... | collective-permute-start | bytes 571400 | tf_op jit(solution)/shard_map/ppermute | solution.py:323
  (75 other events, 695.0 us)
Sparse Core Ops, SparseCore 0:
  11.5 130.3 all-gather.1

commit v2 on v1

--- a/solution.py
+++ b/solution.py
@@ -290,6 +290,7 @@
         self.whole = self.put(other, starts)
         self.known[dim] = 2
         self.piece = None
+        return other
 
     def rows(self):
         return self.whole.reshape((-1,) + self.shape[1:])
@@ -420,13 +421,6 @@
     asked = jnp.sum(jnp.where(owner == position, slot, 0), axis=1)
     turned = (peers[:, None] ^ position) == peers[None, :]
     asked = jnp.sum(jnp.where(turned, asked[None, :], 0), axis=1)
-    paired = jnp.concatenate(
-        [
-            swap(lax.dynamic_slice_in_dim(image_tokens, asked[k], 1), k)
-            for k in range(peer_count)
-        ]
-    )
-
     norm_columns = jnp.pad(jnp.concatenate([norm_gain, norm_bias], axis=1), ((0, 0), (0, 122)))
     rows = self_packed.shape[0]
     ratio = reduce_weight.shape[0] // rows
@@ -442,8 +436,12 @@
     first_group = Gather(
         jnp.concatenate([self_packed, self_output, norm_columns], axis=1), False
     )
-    while first_group.left:
-        first_group.step()
+    while len(first_group.left) > 1:
+        came = first_group.step()
+    wanted = [lax.dynamic_slice_in_dim(image_tokens, asked[k], 1) for k in range(peer_count)]
+    wanted = lax.optimization_barrier((*wanted, came))[:-1]
+    paired = [swap(row, k) for k, row in enumerate(wanted)]
+    first_group.step()
     first_group = first_group.rows()
     packed_weight = first_group[:, : 3 * model_width]
     output_weight = first_group[:, 3 * model_width : 4 * model_width]
@@ -461,6 +459,8 @@
     normed_one = normed_full.astype(jnp.bfloat16)
     packed = project(normed_one, packed_weight).astype(jnp.bfloat16)
     attended = self_forward(packed, caption_lengths)
+    *paired, attended = lax.optimization_barrier((*paired, attended))
+    paired = jnp.concatenate(paired)
     after_self = inputs + project(attended, output_weight)
     normed_full_two, scaled_two, inverse_two = layer_norm(
         after_self, norm_gains[:, 1], norm_shifts[:, 1]

time: 401 us -> 400 us (level)
    ppermute x6, waiting for transfers between devices: 12.7 us -> 1.74 us  [swap(): lax.ppermute(rows, 'seq', [(i, i ^ k) for i in range(lax.axis_size('seq'))])]
    ppermute x5, waiting for transfers between devices: 71.5 us -> 81.1 us  [step(): other = lax.ppermute(self.piece, place[0], swap_pairs(*place))]
    unnamed x149 -> x150, local copies, waits for them, and re-layouts: 16.8 us -> 13.4 us
  transfers between devices with their start and end apart: 37 -> 37, of which waited for: 18 -> 15; matrix products, arithmetic and copies ran while one was open for 25% -> 24% of each run, Pallas kernels for 7% -> 7%
where the time goes in v2:
time: 400 us; the launch traced here: 392 us
  waiting for transfers between devices  127 us (32%)
  local copies, waits for them, and re-layouts  63.2 us (16%)
  Pallas kernels  60.3 us (15%)
  matrix products  44.1 us (11%)
  starting transfers between devices  38.2 us (10%)
  other arithmetic  36.1 us (9%)
  between operations  23.6 us (6%)
    ppermute x5, waiting for transfers between devices, step(): other = lax.ppermute(self.piece, place[0], swap_pairs(*place))  81.1 us
    ppermute x25, waiting for transfers between devices, step(): total = total + lax.ppermute(self.part(places, turn), axis, pairs)  43.7 us
    pallas_call x4, Pallas kernels, attention(): pl.pallas_call(body, grid_spec=pltpu.PrefetchScalarGridSpec(num_scalar_pr...  29.1 us
    ppermute x25, starting transfers between devices, step(): total = total + lax.ppermute(self.part(places, turn), axis, pairs)  27.7 us
    pallas_call x1, Pallas kernels, ffn(): pl.pallas_call(functools.partial(ffn_body, ratio=ratio), grid=(hidden_wid...  25.8 us
    dot_general x5, matrix products, project_back(): lax.dot_general(flat_rows, weight, (((1,), (1,)), ((), ())), preferred_el...  17.4 us
    add x20, other arithmetic, step(): total = total + lax.ppermute(self.part(places, turn), axis, pairs)  16.8 us
    dot_general x5, matrix products, project(): jnp.dot(flat_rows, weight, preferred_element_type=jnp.float32)  16.3 us
  transfers between devices with their start and end apart: 37, of which 15 were waited for; matrix products, arithmetic and copies ran while one was open for 24% of the time, Pallas kernels for 7%

profile of v2, /device:TPU:0, one launch (start us, length us, event | category | flops | bytes accessed | tf_op | source)
XLA Modules:
  0.0 392.0 jit_solution(7642684783593396861)
XLA Ops:
  10.8 4.1 %collective-permute-start = (bf16[1,1,1,1,1,24,3200]{6,5,4,3,2,1,0:T(8,128)(2,1)S(1)}, bf16[1,1,1,1,1,24,3200]{6,5,4,3,2,1,0:T(8,128)(2,1)S(1)}, u32[]{:S(2)}, u32[]{:S(2)}) collective-permute-start(bf16[1,1,1,1,1,24,3200]{6,5,4,3,2,1,0:T(8,128)(2,1)S(1)} %fusion.25), channel_id=1, source_target_pairs={{0,16},{4,20},{8,24},{12,28},{16,0},{20,4},{24,8},{28,12},{1,17},{... | collective-permute-start | bytes 460808 | tf_op jit(solution)/shard_map/ppermute | solution.py:288
  18.1 4.1 %collective-permute-done = bf16[1,1,1,1,1,24,3200]{6,5,4,3,2,1,0:T(8,128)(2,1)S(1)} collective-permute-done((bf16[1,1,1,1,1,24,3200]{6,5,4,3,2,1,0:T(8,128)(2,1)S(1)}, bf16[1,1,1,1,1,24,3200]{6,5,4,3,2,1,0:T(8,128)(2,1)S(1)}, u32[]{:S(2)}, u32[]{:S(2)}) %collective-permute-start) | collective-permute-done | bytes 153632 | tf_op jit(solution)/shard_map/ppermute | solution.py:288
  24.6 16.8 %collective-permute-done.1 = bf16[2,1,1,1,1,24,3200]{6,5,4,3,2,1,0:T(8,128)(2,1)S(1)} collective-permute-done((bf16[2,1,1,1,1,24,3200]{6,5,4,3,2,1,0:T(8,128)(2,1)S(1)}, bf16[2,1,1,1,1,24,3200]{6,5,4,3,2,1,0:T(8,128)(2,1)S(1)}, u32[]{:S(2)}, u32[]{:S(2)}) %collective-permute-start.1) | collective-permute-done | bytes 307232 | tf_op jit(solution)/shard_map/ppermute | solution.py:288
  44.5 24.2 %collective-permute-done.2 = bf16[2,2,1,1,1,24,3200]{6,5,4,3,2,1,0:T(8,128)(2,1)S(1)} collective-permute-done((bf16[2,2,1,1,1,24,3200]{6,5,4,3,2,1,0:T(8,128)(2,1)S(1)}, bf16[2,2,1,1,1,24,3200]{6,5,4,3,2,1,0:T(8,128)(2,1)S(1)}, u32[]{:S(2)}, u32[]{:S(2)}) %collective-permute-start.2) | collective-permute-done | bytes 614432 | tf_op jit(solution)/shard_map/ppermute | solution.py:288
  71.6 36.0 %collective-permute-done.3 = bf16[2,2,2,1,1,24,3200]{6,5,4,3,2,1,0:T(8,128)(2,1)S(1)} collective-permute-done((bf16[2,2,2,1,1,24,3200]{6,5,4,3,2,1,0:T(8,128)(2,1)S(1)}, bf16[2,2,2,1,1,24,3200]{6,5,4,3,2,1,0:T(8,128)(2,1)S(1)}, u32[]{:S(2)}, u32[]{:S(2)}) %collective-permute-start.3) | collective-permute-done | bytes 1228832 | tf_op jit(solution)/shard_map/ppermute | solution.py:288
  108.8 3.4 constant_dynamic-slice_fusion.24
  131.0 3.5 constant_dynamic-update-slice_fusion
  136.8 4.2 %convolution_convert_fusion.query_ref.key_ref.value_ref.refs_1_.refs_2_.refs_3_ = bf16[4,128,2304]{2,1,0:T(8,128)(2,1)S(1)} fusion(bf16[768,3200]{1,0:T(8,128)(2,1)} %bitcast.5, f32[768]{0:T(1024)S(1)} %get-tuple-element.177, f32[768]{0:T(1024)S(1)} %get-tuple-element.178, f32[4,128]{1,0:T(4,128)S(1)} %add_rsqrt_fusion.2, ...), kind=kOutput, calls=%fused_computation.2 | convolution fusion | flops 1815478272 | bytes 6694912 | tf_op jit(solution)/shard_map/dot_general | solution.py:25
  141.0 4.5 %self_attention.1 = bf16[4,128,768]{2,1,0:T(8,128)(2,1)S(1)} custom-call(s32[4]{0:T(128)S(1)} %copy-done.10, bf16[4,128,2304]{2,1,0:T(8,128)(2,1)S(1)} %convolution_convert_fusion.query_ref.key_ref.value_ref.refs_1_.refs_2_.refs_3_, bf16[4,128,2304]{2,1,0:T(8,128)(2,1)S(1)} %convolution_convert_fusion.query_ref.key_ref.value_ref.refs_1_.refs_2_.refs_3_, ...), custom_call_target="tpu_custom_call" | custom-call | flops 201326592 | tf_op jit(solution)/shard_map/self_attention/pallas_call | solution.py:198
  145.6 2.7 fusion.53
  149.9 4.2 %convolution_convert_fusion.1.key_ref.value_ref = bf16[4,196,1536]{2,1,0:T(8,128)(2,1)S(1)} fusion(bf16[4,196,768]{2,1,0:T(8,128)(2,1)} %copy-done.57, bf16[768,9216]{1,0:T(8,128)(2,1)} %all-gather.2.cloned.1.call-done.expand_ref.reduce_ref), kind=kOutput, calls=%fused_computation.7 | convolution fusion | flops 1850892288 | bytes 5996544 | tf_op jit(solution)/shard_map/dot_general | solution.py:25
  154.1 3.1 convolution_convert_fusion.6.query_ref
  157.2 4.1 %cross_attention.1 = bf16[4,128,768]{2,1,0:T(8,128)(2,1)S(1)} custom-call(s32[4]{0:T(128)S(1)} %broadcast_xor_fusion.table_ref, bf16[4,128,768]{2,1,0:T(8,128)(2,1)S(1)} %convolution_convert_fusion.6.query_ref, bf16[4,196,1536]{2,1,0:T(8,128)(2,1)S(1)} %convolution_convert_fusion.1.key_ref.value_ref, ...), custom_call_target="tpu_custom_call" | custom-call | flops 308281344 | tf_op jit(solution)/shard_map/cross_attention/pallas_call | solution.py:198
  165.4 25.8 %ffn.1 = (f32[512,768]{1,0:T(8,128)S(1)}, f32[512,768]{1,0:T(8,128)S(1)}, bf16[3072,768]{1,0:T(8,128)(2,1)}, bf16[768,3072]{1,0:T(8,128)(2,1)}) custom-call(bf16[512,768]{1,0:T(8,128)(2,1)S(1)} %bitcast.110, bf16[512,768]{1,0:T(8,128)(2,1)S(1)} %bitcast.109, bf16[768,9216]{1,0:T(8,128)(2,1)} %all-gather.2.cloned.1.call-done.expand_ref.reduce_ref, ...), custom_call_target="tpu_custom_call" | custom-call | tf_op jit(solution)/shard_map/ffn/pallas_call | solution.py:103
  191.2 4.4 %constant_dynamic-slice_fusion.23 = bf16[2,2,2,2,1,96,768]{6,5,4,3,2,1,0:T(8,128)(2,1)} fusion(bf16[2,2,2,2,2,96,768]{6,5,4,3,2,1,0:T(8,128)(2,1)} %bitcast.120, s32[]{:T(128)S(6)} %select_n.225), kind=kLoop, calls=%fused_computation.127 | loop fusion | bytes 4718596 | tf_op jit(solution)/shard_map/dynamic_slice | solution.py:314
  203.6 2.9 convolution_convert_fusion.4.grad_ref
  215.5 11.8 %cross_backward.1 = (bf16[4,128,768]{2,1,0:T(8,128)(2,1)S(1)}, bf16[4,196,1536]{2,1,0:T(8,128)(2,1)S(1)}) custom-call(s32[4]{0:T(128)S(1)} %broadcast_xor_fusion.table_ref, bf16[4,128,768]{2,1,0:T(8,128)(2,1)S(1)} %copy-done.4, bf16[4,196,1536]{2,1,0:T(8,128)(2,1)} %copy-done, bf16[4,196,1536]{2,1,0:T(8,128)(2,1)} %copy-done, ...), custom_call_target="tpu_custom_call" | custom-call | flops 770703360 | tf_op jit(solution)/shard_map/cross_backward/pallas_call | solution.py:198
  227.4 2.9 bitcast_convert_fusion.1
  231.4 6.1 %fusion.21 = bf16[4,196,768]{2,1,0:T(8,128)(2,1)} fusion(bf16[4,196,1536]{2,1,0:T(8,128)(2,1)S(1)} %get-tuple-element.80, bf16[768,9216]{1,0:T(8,128)(2,1)} %all-gather.2.cloned.1.call-done.expand_ref.reduce_ref), kind=kOutput, calls=%fused_computation.58 | convolution fusion | flops 1850290176 | bytes 5971968 | tf_op jit(solution)/shard_map/dot_general | solution.py:32
  237.5 3.5 collective-permute-done.10
  273.2 8.7 %self_backward.1 = bf16[4,128,2304]{2,1,0:T(8,128)(2,1)S(1)} custom-call(s32[4]{0:T(128)S(1)} %copy-done.10, bf16[4,128,2304]{2,1,0:T(8,128)(2,1)S(1)} %convolution_convert_fusion.query_ref.key_ref.value_ref.refs_1_.refs_2_.refs_3_, bf16[4,128,2304]{2,1,0:T(8,128)(2,1)S(1)} %convolution_convert_fusion.query_ref.key_ref.value_ref.refs_1_.refs_2_.refs_3_, ...), custom_call_target="tpu_custom_call" | custom-call | flops 503316480 | tf_op jit(solution)/shard_map/self_backward/pallas_call | solution.py:198
  282.6 6.7 %collective-permute-done.17 = bf16[2,2,1,2,1,24,2304]{6,5,4,3,2,1,0:T(8,128)(2,1)S(1)} collective-permute-done((bf16[2,2,1,2,1,24,2304]{6,5,4,3,2,1,0:T(8,128)(2,1)S(1)}, bf16[2,2,1,2,1,24,2304]{6,5,4,3,2,1,0:T(8,128)(2,1)S(1)}, u32[]{:S(2)}, u32[]{:S(2)}) %collective-permute-start.17) | collective-permute-done | bytes 884768 | tf_op jit(solution)/shard_map/ppermute | solution.py:324
  295.2 4.0 %fusion.1 = f32[512,768]{1,0:T(8,128)S(1)} fusion(bf16[512,2304]{1,0:T(8,128)(2,1)S(1)} %bitcast.111, bf16[768,3200]{1,0:T(8,128)(2,1)} %bitcast.5), kind=kOutput, calls=%fused_computation.8 | convolution fusion | flops 1811939328 | bytes 7471104 | tf_op jit(solution)/shard_map/dot_general | solution.py:32
  303.5 7.1 %collective-permute-start.22 = (bf16[1,1,1,1,1,96,768]{6,5,4,3,2,1,0:T(8,128)(2,1)}, bf16[1,1,1,1,1,96,768]{6,5,4,3,2,1,0:T(8,128)(2,1)}, u32[]{:S(2)}, u32[]{:S(2)}) collective-permute-start(bf16[1,1,1,1,1,96,768]{6,5,4,3,2,1,0:T(8,128)(2,1)} %constant_dynamic-slice_fusion.12), channel_id=1, source_target_pairs={{0,16},{4,20},{8,24},{12,28},{16,0},{20,4},{24,8},{28,12},{1,17},{... | collective-permute-start | bytes 442376 | tf_op jit(solution)/shard_map/ppermute | solution.py:324
  329.5 3.6 collective-permute-start.28
  337.3 3.1 collective-permute-done.27
  341.8 9.9 %collective-permute-done.29 = bf16[2,2,1,2,1,24,1920]{6,5,4,3,2,1,0:T(8,128)(2,1)S(1)} collective-permute-done((bf16[2,2,1,2,1,24,1920]{6,5,4,3,2,1,0:T(8,128)(2,1)S(1)}, bf16[2,2,1,2,1,24,1920]{6,5,4,3,2,1,0:T(8,128)(2,1)S(1)}, u32[]{:S(2)}, u32[]{:S(2)}) %collective-permute-start.29) | collective-permute-done | bytes 737312 | tf_op jit(solution)/shard_map/ppermute | solution.py:324
  357.2 7.2 %collective-permute-done.31 = bf16[2,2,1,1,1,24,1920]{6,5,4,3,2,1,0:T(8,128)(2,1)S(1)} collective-permute-done((bf16[2,2,1,1,1,24,1920]{6,5,4,3,2,1,0:T(8,128)(2,1)S(1)}, bf16[2,2,1,1,1,24,1920]{6,5,4,3,2,1,0:T(8,128)(2,1)S(1)}, u32[]{:S(2)}, u32[]{:S(2)}) %collective-permute-start.31) | collective-permute-done | bytes 368672 | tf_op jit(solution)/shard_map/ppermute | solution.py:324
  364.7 3.5 collective-permute-start.35
  369.9 3.6 put_rows.1
  373.5 2.8 copy.77
  376.3 5.6 %collective-permute-done.33 = bf16[1,1,1,1,1,24,3968]{6,5,4,3,2,1,0:T(8,128)(2,1)S(1)} collective-permute-done((bf16[1,1,1,1,1,24,3968]{6,5,4,3,2,1,0:T(8,128)(2,1)S(1)}, bf16[1,1,1,1,1,24,3968]{6,5,4,3,2,1,0:T(8,128)(2,1)S(1)}, u32[]{:S(2)}, u32[]{:S(2)}) %collective-permute-start.33) | collective-permute-done | bytes 190496 | tf_op jit(solution)/shard_map/ppermute | solution.py:324
  (341 shorter events, 130.3 us)
Async XLA Ops:
  7.2 142.6 %all-gather.2.cloned.1.call-start = ((), (), s32[]{:S(2)}) async-start(), calls=%async_computation | async-start | bytes 14598144 | tf_op jit(solution)/shard_map/all_gather | solution.py:428
  10.8 11.4 %collective-permute-start = (bf16[1,1,1,1,1,24,3200]{6,5,4,3,2,1,0:T(8,128)(2,1)S(1)}, bf16[1,1,1,1,1,24,3200]{6,5,4,3,2,1,0:T(8,128)(2,1)S(1)}, u32[]{:S(2)}, u32[]{:S(2)}) collective-permute-start(bf16[1,1,1,1,1,24,3200]{6,5,4,3,2,1,0:T(8,128)(2,1)S(1)} %fusion.25), channel_id=1, source_target_pairs={{0,16},{4,20},{8,24},{12,28},{16,0},{20,4},{24,8},{28,12},{1,17},{... | collective-permute-start | bytes 460808 | tf_op jit(solution)/shard_map/ppermute | solution.py:288
  23.9 17.6 %collective-permute-start.1 = (bf16[2,1,1,1,1,24,3200]{6,5,4,3,2,1,0:T(8,128)(2,1)S(1)}, bf16[2,1,1,1,1,24,3200]{6,5,4,3,2,1,0:T(8,128)(2,1)S(1)}, u32[]{:S(2)}, u32[]{:S(2)}) collective-permute-start(bf16[2,1,1,1,1,24,3200]{6,5,4,3,2,1,0:T(8,128)(2,1)S(1)} %constant_dynamic-slice_fusion.27), channel_id=1, source_target_pairs={{0,8},{4,12},{8,0},{12,4},{16,24},{20,28},{24,16},{28,20},{1,9},{5... | collective-permute-start | bytes 921608 | tf_op jit(solution)/shard_map/ppermute | solution.py:288
  43.3 25.3 %collective-permute-start.2 = (bf16[2,2,1,1,1,24,3200]{6,5,4,3,2,1,0:T(8,128)(2,1)S(1)}, bf16[2,2,1,1,1,24,3200]{6,5,4,3,2,1,0:T(8,128)(2,1)S(1)}, u32[]{:S(2)}, u32[]{:S(2)}) collective-permute-start(bf16[2,2,1,1,1,24,3200]{6,5,4,3,2,1,0:T(8,128)(2,1)S(1)} %constant_dynamic-slice_fusion.26), channel_id=1, source_target_pairs={{0,4},{4,0},{8,12},{12,8},{16,20},{20,16},{24,28},{28,24},{1,5},{5... | collective-permute-start | bytes 1843208 | tf_op jit(solution)/shard_map/ppermute | solution.py:288
  70.9 36.7 %collective-permute-start.3 = (bf16[2,2,2,1,1,24,3200]{6,5,4,3,2,1,0:T(8,128)(2,1)S(1)}, bf16[2,2,2,1,1,24,3200]{6,5,4,3,2,1,0:T(8,128)(2,1)S(1)}, u32[]{:S(2)}, u32[]{:S(2)}) collective-permute-start(bf16[2,2,2,1,1,24,3200]{6,5,4,3,2,1,0:T(8,128)(2,1)S(1)} %constant_dynamic-slice_fusion.25), channel_id=1, source_target_pairs={{0,2},{1,3},{2,0},{3,1},{4,6},{5,7},{6,4},{7,5},{8,10},{9,11},{10,... | collective-permute-start | bytes 3686408 | tf_op jit(solution)/shard_map/ppermute | solution.py:288
  112.2 18.8 %collective-permute-start.7 = (bf16[2,2,2,2,1,24,3200]{6,5,4,3,2,1,0:T(8,128)(2,1)}, bf16[2,2,2,2,1,24,3200]{6,5,4,3,2,1,0:T(8,128)(2,1)}, u32[]{:S(2)}, u32[]{:S(2)}) collective-permute-start(bf16[2,2,2,2,1,24,3200]{6,5,4,3,2,1,0:T(8,128)(2,1)} %constant_dynamic-slice_fusion.24), channel_id=1, source_target_pairs={{0,1},{1,0},{2,3},{3,2},{4,5},{5,4},{6,7},{7,6},{8,9},{9,8},{10,11... | collective-permute-start | bytes 7372808 | tf_op jit(solution)/shard_map/ppermute | solution.py:288
  129.1 16.3 %collective-permute-start.4 = (bf16[1,196,768]{2,1,0:T(8,128)(2,1)}, bf16[1,196,768]{2,1,0:T(8,128)(2,1)S(1)}, u32[]{:S(2)}, u32[]{:S(2)}) collective-permute-start(bf16[1,196,768]{2,1,0:T(8,128)(2,1)} %copy.85), channel_id=1, source_target_pairs={{0,1},{1,0},{2,3},{3,2},{4,5},{5,4},{6,7},{7,6},{8,9},{9,8},{10,11... | collective-permute-start | bytes 903176 | tf_op jit(solution)/shard_map/ppermute | solution.py:350
  129.6 15.8 %collective-permute-start.5 = (bf16[1,196,768]{2,1,0:T(8,128)(2,1)}, bf16[1,196,768]{2,1,0:T(8,128)(2,1)S(1)}, u32[]{:S(2)}, u32[]{:S(2)}) collective-permute-start(bf16[1,196,768]{2,1,0:T(8,128)(2,1)} %copy.86), channel_id=1, source_target_pairs={{0,2},{1,3},{2,0},{3,1},{4,6},{5,7},{6,4},{7,5},{8,10},{9,11},{10,... | collective-permute-start | bytes 903176 | tf_op jit(solution)/shard_map/ppermute | solution.py:350
  130.2 15.3 %collective-permute-start.6 = (bf16[1,196,768]{2,1,0:T(8,128)(2,1)}, bf16[1,196,768]{2,1,0:T(8,128)(2,1)S(1)}, u32[]{:S(2)}, u32[]{:S(2)}) collective-permute-start(bf16[1,196,768]{2,1,0:T(8,128)(2,1)} %copy.87), channel_id=1, source_target_pairs={{0,3},{1,2},{2,1},{3,0},{4,7},{5,6},{6,5},{7,4},{8,11},{9,10},{10,... | collective-permute-start | bytes 903176 | tf_op jit(solution)/shard_map/ppermute | solution.py:350
  195.6 12.0 %collective-permute-start.8 = (bf16[2,2,2,2,1,96,768]{6,5,4,3,2,1,0:T(8,128)(2,1)}, bf16[2,2,2,2,1,96,768]{6,5,4,3,2,1,0:T(8,128)(2,1)}, u32[]{:S(2)}, u32[]{:S(2)}) collective-permute-start(bf16[2,2,2,2,1,96,768]{6,5,4,3,2,1,0:T(8,128)(2,1)} %constant_dynamic-slice_fusion.23), channel_id=1, source_target_pairs={{0,1},{1,0},{2,3},{3,2},{4,5},{5,4},{6,7},{7,6},{8,9},{9,8},{10,11... | collective-permute-start | bytes 7077896 | tf_op jit(solution)/shard_map/ppermute | solution.py:324
  197.9 11.7 %collective-permute-start.9 = (bf16[2,2,2,2,1,24,3072]{6,5,4,3,2,1,0:T(8,128)(2,1)}, bf16[2,2,2,2,1,24,3072]{6,5,4,3,2,1,0:T(8,128)(2,1)}, u32[]{:S(2)}, u32[]{:S(2)}) collective-permute-start(bf16[2,2,2,2,1,24,3072]{6,5,4,3,2,1,0:T(8,128)(2,1)} %constant_dynamic-slice_fusion.22), channel_id=1, source_target_pairs={{0,1},{1,0},{2,3},{3,2},{4,5},{5,4},{6,7},{7,6},{8,9},{9,8},{10,11... | collective-permute-start | bytes 7077896 | tf_op jit(solution)/shard_map/ppermute | solution.py:324
  212.8 28.2 %collective-permute-start.10 = (bf16[2,2,1,2,1,96,768]{6,5,4,3,2,1,0:T(8,128)(2,1)}, bf16[2,2,1,2,1,96,768]{6,5,4,3,2,1,0:T(8,128)(2,1)}, u32[]{:S(2)}, u32[]{:S(2)}) collective-permute-start(bf16[2,2,1,2,1,96,768]{6,5,4,3,2,1,0:T(8,128)(2,1)} %constant_dynamic-slice_fusion.21), channel_id=1, source_target_pairs={{0,4},{4,0},{8,12},{12,8},{16,20},{20,16},{24,28},{28,24},{1,5},{5... | collective-permute-start | bytes 3538952 | tf_op jit(solution)/shard_map/ppermute | solution.py:324
  214.0 28.4 %collective-permute-start.11 = (bf16[2,2,2,1,1,24,3072]{6,5,4,3,2,1,0:T(8,128)(2,1)}, bf16[2,2,2,1,1,24,3072]{6,5,4,3,2,1,0:T(8,128)(2,1)}, u32[]{:S(2)}, u32[]{:S(2)}) collective-permute-start(bf16[2,2,2,1,1,24,3072]{6,5,4,3,2,1,0:T(8,128)(2,1)} %constant_dynamic-slice_fusion.20), channel_id=1, source_target_pairs={{0,2},{1,3},{2,0},{3,1},{4,6},{5,7},{6,4},{7,5},{8,10},{9,11},{10,... | collective-permute-start | bytes 3538952 | tf_op jit(solution)/shard_map/ppermute | solution.py:324
  245.2 16.1 %collective-permute-start.12 = (bf16[2,2,1,1,1,96,768]{6,5,4,3,2,1,0:T(8,128)(2,1)}, bf16[2,2,1,1,1,96,768]{6,5,4,3,2,1,0:T(8,128)(2,1)}, u32[]{:S(2)}, u32[]{:S(2)}) collective-permute-start(bf16[2,2,1,1,1,96,768]{6,5,4,3,2,1,0:T(8,128)(2,1)} %constant_dynamic-slice_fusion.19), channel_id=1, source_target_pairs={{0,2},{1,3},{2,0},{3,1},{4,6},{5,7},{6,4},{7,5},{8,10},{9,11},{10,... | collective-permute-start | bytes 1769480 | tf_op jit(solution)/shard_map/ppermute | solution.py:324
  246.7 16.0 %collective-permute-start.13 = (bf16[2,2,1,1,1,24,3072]{6,5,4,3,2,1,0:T(8,128)(2,1)}, bf16[2,2,1,1,1,24,3072]{6,5,4,3,2,1,0:T(8,128)(2,1)}, u32[]{:S(2)}, u32[]{:S(2)}) collective-permute-start(bf16[2,2,1,1,1,24,3072]{6,5,4,3,2,1,0:T(8,128)(2,1)} %constant_dynamic-slice_fusion.18), channel_id=1, source_target_pairs={{0,4},{4,0},{8,12},{12,8},{16,20},{20,16},{24,28},{28,24},{1,5},{5... | collective-permute-start | bytes 1769480 | tf_op jit(solution)/shard_map/ppermute | solution.py:324
  249.1 14.7 %collective-permute-start.14 = (bf16[2,2,2,2,1,24,2304]{6,5,4,3,2,1,0:T(8,128)(2,1)}, bf16[2,2,2,2,1,24,2304]{6,5,4,3,2,1,0:T(8,128)(2,1)}, u32[]{:S(2)}, u32[]{:S(2)}) collective-permute-start(bf16[2,2,2,2,1,24,2304]{6,5,4,3,2,1,0:T(8,128)(2,1)} %constant_dynamic-slice_fusion.17), channel_id=1, source_target_pairs={{0,1},{1,0},{2,3},{3,2},{4,5},{5,4},{6,7},{7,6},{8,9},{9,8},{10,11... | collective-permute-start | bytes 5308424 | tf_op jit(solution)/shard_map/ppermute | solution.py:324
  265.6 16.4 %collective-permute-start.15 = (bf16[2,1,1,1,1,96,768]{6,5,4,3,2,1,0:T(8,128)(2,1)S(1)}, bf16[2,1,1,1,1,96,768]{6,5,4,3,2,1,0:T(8,128)(2,1)S(1)}, u32[]{:S(2)}, u32[]{:S(2)}) collective-permute-start(bf16[2,1,1,1,1,96,768]{6,5,4,3,2,1,0:T(8,128)(2,1)S(1)} %constant_dynamic-slice_fusion.16), channel_id=1, source_target_pairs={{0,8},{4,12},{8,0},{12,4},{16,24},{20,28},{24,16},{28,20},{1,9},{5... | collective-permute-start | bytes 884744 | tf_op jit(solution)/shard_map/ppermute | solution.py:324
  265.7 16.9 %collective-permute-start.16 = (bf16[2,1,1,1,1,24,3072]{6,5,4,3,2,1,0:T(8,128)(2,1)S(1)}, bf16[2,1,1,1,1,24,3072]{6,5,4,3,2,1,0:T(8,128)(2,1)S(1)}, u32[]{:S(2)}, u32[]{:S(2)}) collective-permute-start(bf16[2,1,1,1,1,24,3072]{6,5,4,3,2,1,0:T(8,128)(2,1)S(1)} %constant_dynamic-slice_fusion.15), channel_id=1, source_target_pairs={{0,8},{4,12},{8,0},{12,4},{16,24},{20,28},{24,16},{28,20},{1,9},{5... | collective-permute-start | bytes 884744 | tf_op jit(solution)/shard_map/ppermute | solution.py:324
  267.8 21.5 %collective-permute-start.17 = (bf16[2,2,1,2,1,24,2304]{6,5,4,3,2,1,0:T(8,128)(2,1)S(1)}, bf16[2,2,1,2,1,24,2304]{6,5,4,3,2,1,0:T(8,128)(2,1)S(1)}, u32[]{:S(2)}, u32[]{:S(2)}) collective-permute-start(bf16[2,2,1,2,1,24,2304]{6,5,4,3,2,1,0:T(8,128)(2,1)S(1)} %constant_dynamic-slice_fusion.14), channel_id=1, source_target_pairs={{0,4},{4,0},{8,12},{12,8},{16,20},{20,16},{24,28},{28,24},{1,5},{5... | collective-permute-start | bytes 2654216 | tf_op jit(solution)/shard_map/ppermute | solution.py:324
  271.8 17.6 %collective-permute-start.18 = (bf16[1,196,768]{2,1,0:T(8,128)(2,1)S(1)}, bf16[1,196,768]{2,1,0:T(8,128)(2,1)S(1)}, u32[]{:S(2)}, u32[]{:S(2)}) collective-permute-start(bf16[1,196,768]{2,1,0:T(8,128)(2,1)S(1)} %get-tuple-element.187), channel_id=1, source_target_pairs={{0,1},{1,0},{2,3},{3,2},{4,5},{5,4},{6,7},{7,6},{8,9},{9,8},{10,11... | collective-permute-start | bytes 903176 | tf_op jit(solution)/shard_map/ppermute | solution.py:350
  271.8 17.6 %collective-permute-start.19 = (bf16[1,196,768]{2,1,0:T(8,128)(2,1)S(1)}, bf16[1,196,768]{2,1,0:T(8,128)(2,1)S(1)}, u32[]{:S(2)}, u32[]{:S(2)}) collective-permute-start(bf16[1,196,768]{2,1,0:T(8,128)(2,1)S(1)} %get-tuple-element.186), channel_id=1, source_target_pairs={{0,2},{1,3},{2,0},{3,1},{4,6},{5,7},{6,4},{7,5},{8,10},{9,11},{10,... | collective-permute-start | bytes 903176 | tf_op jit(solution)/shard_map/ppermute | solution.py:350
  282.0 9.2 %collective-permute-start.20 = (bf16[1,196,768]{2,1,0:T(8,128)(2,1)S(1)}, bf16[1,196,768]{2,1,0:T(8,128)(2,1)S(1)}, u32[]{:S(2)}, u32[]{:S(2)}) collective-permute-start(bf16[1,196,768]{2,1,0:T(8,128)(2,1)S(1)} %get-tuple-element.185), channel_id=1, source_target_pairs={{0,3},{1,2},{2,1},{3,0},{4,7},{5,6},{6,5},{7,4},{8,11},{9,10},{10,... | collective-permute-start | bytes 903176 | tf_op jit(solution)/shard_map/ppermute | solution.py:350
  302.2 24.1 %collective-permute-start.21 = (bf16[2,2,1,1,1,24,2304]{6,5,4,3,2,1,0:T(8,128)(2,1)}, bf16[2,2,1,1,1,24,2304]{6,5,4,3,2,1,0:T(8,128)(2,1)}, u32[]{:S(2)}, u32[]{:S(2)}) collective-permute-start(bf16[2,2,1,1,1,24,2304]{6,5,4,3,2,1,0:T(8,128)(2,1)} %constant_dynamic-slice_fusion.13), channel_id=1, source_target_pairs={{0,2},{1,3},{2,0},{3,1},{4,6},{5,7},{6,4},{7,5},{8,10},{9,11},{10,... | collective-permute-start | bytes 1327112 | tf_op jit(solution)/shard_map/ppermute | solution.py:324
  303.5 21.8 %collective-permute-start.22 = (bf16[1,1,1,1,1,96,768]{6,5,4,3,2,1,0:T(8,128)(2,1)}, bf16[1,1,1,1,1,96,768]{6,5,4,3,2,1,0:T(8,128)(2,1)}, u32[]{:S(2)}, u32[]{:S(2)}) collective-permute-start(bf16[1,1,1,1,1,96,768]{6,5,4,3,2,1,0:T(8,128)(2,1)} %constant_dynamic-slice_fusion.12), channel_id=1, source_target_pairs={{0,16},{4,20},{8,24},{12,28},{16,0},{20,4},{24,8},{28,12},{1,17},{... | collective-permute-start | bytes 442376 | tf_op jit(solution)/shard_map/ppermute | solution.py:324
  311.3 13.1 %collective-permute-start.23 = (bf16[1,1,1,1,1,24,3072]{6,5,4,3,2,1,0:T(8,128)(2,1)}, bf16[1,1,1,1,1,24,3072]{6,5,4,3,2,1,0:T(8,128)(2,1)}, u32[]{:S(2)}, u32[]{:S(2)}) collective-permute-start(bf16[1,1,1,1,1,24,3072]{6,5,4,3,2,1,0:T(8,128)(2,1)} %constant_dynamic-slice_fusion.11), channel_id=1, source_target_pairs={{0,16},{4,20},{8,24},{12,28},{16,0},{20,4},{24,8},{28,12},{1,17},{... | collective-permute-start | bytes 442376 | tf_op jit(solution)/shard_map/ppermute | solution.py:324
  314.3 13.0 %collective-permute-start.24 = (bf16[2,2,2,2,1,24,1920]{6,5,4,3,2,1,0:T(8,128)(2,1)}, bf16[2,2,2,2,1,24,1920]{6,5,4,3,2,1,0:T(8,128)(2,1)}, u32[]{:S(2)}, u32[]{:S(2)}) collective-permute-start(bf16[2,2,2,2,1,24,1920]{6,5,4,3,2,1,0:T(8,128)(2,1)} %constant_dynamic-slice_fusion.10), channel_id=1, source_target_pairs={{0,1},{1,0},{2,3},{3,2},{4,5},{5,4},{6,7},{7,6},{8,9},{9,8},{10,11... | collective-permute-start | bytes 4423688 | tf_op jit(solution)/shard_map/ppermute | solution.py:324
  318.4 10.6 %collective-permute-start.25 = (bf16[2,2,2,2,1,24,2048]{6,5,4,3,2,1,0:T(8,128)(2,1)S(1)}, bf16[2,2,2,2,1,24,2048]{6,5,4,3,2,1,0:T(8,128)(2,1)S(1)}, u32[]{:S(2)}, u32[]{:S(2)}) collective-permute-start(bf16[2,2,2,2,1,24,2048]{6,5,4,3,2,1,0:T(8,128)(2,1)S(1)} %fusion.16), channel_id=1, source_target_pairs={{0,1},{1,0},{2,3},{3,2},{4,5},{5,4},{6,7},{7,6},{8,9},{9,8},{10,11... | collective-permute-start | bytes 4718600 | tf_op jit(solution)/shard_map/ppermute | solution.py:324
  334.0 17.6 %collective-permute-start.29 = (bf16[2,2,1,2,1,24,1920]{6,5,4,3,2,1,0:T(8,128)(2,1)S(1)}, bf16[2,2,1,2,1,24,1920]{6,5,4,3,2,1,0:T(8,128)(2,1)S(1)}, u32[]{:S(2)}, u32[]{:S(2)}) collective-permute-start(bf16[2,2,1,2,1,24,1920]{6,5,4,3,2,1,0:T(8,128)(2,1)S(1)} %constant_dynamic-slice_fusion.6), channel_id=1, source_target_pairs={{0,4},{4,0},{8,12},{12,8},{16,20},{20,16},{24,28},{28,24},{1,5},{5... | collective-permute-start | bytes 2211848 | tf_op jit(solution)/shard_map/ppermute | solution.py:324
  335.2 18.4 %collective-permute-start.30 = (bf16[2,2,2,1,1,24,2048]{6,5,4,3,2,1,0:T(8,128)(2,1)S(1)}, bf16[2,2,2,1,1,24,2048]{6,5,4,3,2,1,0:T(8,128)(2,1)S(1)}, u32[]{:S(2)}, u32[]{:S(2)}) collective-permute-start(bf16[2,2,2,1,1,24,2048]{6,5,4,3,2,1,0:T(8,128)(2,1)S(1)} %constant_dynamic-slice_fusion.5), channel_id=1, source_target_pairs={{0,2},{1,3},{2,0},{3,1},{4,6},{5,7},{6,4},{7,5},{8,10},{9,11},{10,... | collective-permute-start | bytes 2359304 | tf_op jit(solution)/shard_map/ppermute | solution.py:324
  355.0 9.5 %collective-permute-start.32 = (bf16[2,2,1,1,1,24,2048]{6,5,4,3,2,1,0:T(8,128)(2,1)S(1)}, bf16[2,2,1,1,1,24,2048]{6,5,4,3,2,1,0:T(8,128)(2,1)S(1)}, u32[]{:S(2)}, u32[]{:S(2)}) collective-permute-start(bf16[2,2,1,1,1,24,2048]{6,5,4,3,2,1,0:T(8,128)(2,1)S(1)} %constant_dynamic-slice_fusion.3), channel_id=1, source_target_pairs={{0,4},{4,0},{8,12},{12,8},{16,20},{20,16},{24,28},{28,24},{1,5},{5... | collective-permute-start | bytes 1179656 | tf_op jit(solution)/shard_map/ppermute | solution.py:324
  364.7 11.5 %collective-permute-start.35 = (bf16[1,1,1,1,1,24,3968]{6,5,4,3,2,1,0:T(8,128)(2,1)S(1)}, bf16[1,1,1,1,1,24,3968]{6,5,4,3,2,1,0:T(8,128)(2,1)S(1)}, u32[]{:S(2)}, u32[]{:S(2)}) collective-permute-start(bf16[1,1,1,1,1,24,3968]{6,5,4,3,2,1,0:T(8,128)(2,1)S(1)} %get-tuple-element.196), channel_id=1, source_target_pairs={{0,24},{4,28},{8,16},{12,20},{16,8},{20,12},{24,0},{28,4},{1,25},{... | collective-permute-start | bytes 571400 | tf_op jit(solution)/shard_map/ppermute | solution.py:324
  368.2 13.7 %collective-permute-start.33 = (bf16[1,1,1,1,1,24,3968]{6,5,4,3,2,1,0:T(8,128)(2,1)S(1)}, bf16[1,1,1,1,1,24,3968]{6,5,4,3,2,1,0:T(8,128)(2,1)S(1)}, u32[]{:S(2)}, u32[]{:S(2)}) collective-permute-start(bf16[1,1,1,1,1,24,3968]{6,5,4,3,2,1,0:T(8,128)(2,1)S(1)} %get-tuple-element.195), channel_id=1, source_target_pairs={{0,16},{4,20},{8,24},{12,28},{16,0},{20,4},{24,8},{28,12},{1,17},{... | collective-permute-start | bytes 571400 | tf_op jit(solution)/shard_map/ppermute | solution.py:324
  (77 other events, 694.1 us)
Sparse Core Ops, SparseCore 0:
  11.5 123.5 all-gather.1

commit v3 on v2

--- a/solution.py
+++ b/solution.py
@@ -436,9 +436,13 @@
     first_group = Gather(
         jnp.concatenate([self_packed, self_output, norm_columns], axis=1), False
     )
+    first_group.step()
+    first_group.whole, asked, place = lax.optimization_barrier((first_group.whole, asked, place))
+    first_group.step()
+    wanted = [lax.dynamic_slice_in_dim(image_tokens, asked[k], 1) for k in range(peer_count)]
+    first_group.whole, *wanted = lax.optimization_barrier((first_group.whole, *wanted))
     while len(first_group.left) > 1:
         came = first_group.step()
-    wanted = [lax.dynamic_slice_in_dim(image_tokens, asked[k], 1) for k in range(peer_count)]
     wanted = lax.optimization_barrier((*wanted, came))[:-1]
     paired = [swap(row, k) for k, row in enumerate(wanted)]
     first_group.step()

time: 400 us -> 387 us (0.968)
  waiting for transfers between devices: 127 us -> 114 us
  local copies, waits for them, and re-layouts: 63.2 us -> 67.9 us
    ppermute x5, waiting for transfers between devices: 81.1 us -> 68.5 us  [step(): other = lax.ppermute(self.piece, place[0], swap_pairs(*place))]
    unnamed x150 -> x164, local copies, waits for them, and re-layouts: 13.4 us -> 18.6 us
  transfers between devices with their start and end apart: 37 -> 37, of which waited for: 15 -> 18; matrix products, arithmetic and copies ran while one was open for 24% -> 25% of each run, Pallas kernels for 7% -> 8%
where the time goes in v3:
time: 387 us; the launch traced here: 379 us
  waiting for transfers between devices  114 us (29%)
  local copies, waits for them, and re-layouts  67.9 us (18%)
  Pallas kernels  60.3 us (16%)
  matrix products  42.9 us (11%)
  other arithmetic  35.7 us (9%)
  starting transfers between devices  35.3 us (9%)
  between operations  23.5 us (6%)
    ppermute x5, waiting for transfers between devices, step(): other = lax.ppermute(self.piece, place[0], swap_pairs(*place))  68.5 us
    ppermute x25, waiting for transfers between devices, step(): total = total + lax.ppermute(self.part(places, turn), axis, pairs)  41.1 us
    pallas_call x4, Pallas kernels, attention(): pl.pallas_call(body, grid_spec=pltpu.PrefetchScalarGridSpec(num_scalar_pr...  29.1 us
    pallas_call x1, Pallas kernels, ffn(): pl.pallas_call(functools.partial(ffn_body, ratio=ratio), grid=(hidden_wid...  25.8 us
    ppermute x25, starting transfers between devices, step(): total = total + lax.ppermute(self.part(places, turn), axis, pairs)  24.9 us
    unnamed x164, local copies, waits for them, and re-layouts  18.6 us
    add x20, other arithmetic, step(): total = total + lax.ppermute(self.part(places, turn), axis, pairs)  17.2 us
    dot_general x5, matrix products, project(): jnp.dot(flat_rows, weight, preferred_element_type=jnp.float32)  16.1 us
  transfers between devices with their start and end apart: 37, of which 18 were waited for; matrix products, arithmetic and copies ran while one was open for 25% of the time, Pallas kernels for 8%

profile of v3, /device:TPU:0, one launch (start us, length us, event | category | flops | bytes accessed | tf_op | source)
XLA Modules:
  0.0 379.5 jit_solution(202169859847750908)
XLA Ops:
  10.8 4.1 %collective-permute-start = (bf16[1,1,1,1,1,24,3200]{6,5,4,3,2,1,0:T(8,128)(2,1)S(1)}, bf16[1,1,1,1,1,24,3200]{6,5,4,3,2,1,0:T(8,128)(2,1)S(1)}, u32[]{:S(2)}, u32[]{:S(2)}) collective-permute-start(bf16[1,1,1,1,1,24,3200]{6,5,4,3,2,1,0:T(8,128)(2,1)S(1)} %fusion.25), channel_id=1, source_target_pairs={{0,16},{4,20},{8,24},{12,28},{16,0},{20,4},{24,8},{28,12},{1,17},{... | collective-permute-start | bytes 460808 | tf_op jit(solution)/shard_map/ppermute | solution.py:288
  18.0 4.2 %collective-permute-done = bf16[1,1,1,1,1,24,3200]{6,5,4,3,2,1,0:T(8,128)(2,1)S(1)} collective-permute-done((bf16[1,1,1,1,1,24,3200]{6,5,4,3,2,1,0:T(8,128)(2,1)S(1)}, bf16[1,1,1,1,1,24,3200]{6,5,4,3,2,1,0:T(8,128)(2,1)S(1)}, u32[]{:S(2)}, u32[]{:S(2)}) %collective-permute-start) | collective-permute-done | bytes 153632 | tf_op jit(solution)/shard_map/ppermute | solution.py:288
  33.0 2.5 constant_dynamic-slice_fusion.27
  38.7 2.8 collective-permute-done.1
  44.5 24.1 %collective-permute-done.2 = bf16[2,2,1,1,1,24,3200]{6,5,4,3,2,1,0:T(8,128)(2,1)S(1)} collective-permute-done((bf16[2,2,1,1,1,24,3200]{6,5,4,3,2,1,0:T(8,128)(2,1)S(1)}, bf16[2,2,1,1,1,24,3200]{6,5,4,3,2,1,0:T(8,128)(2,1)S(1)}, u32[]{:S(2)}, u32[]{:S(2)}) %collective-permute-start.2) | collective-permute-done | bytes 614432 | tf_op jit(solution)/shard_map/ppermute | solution.py:288
  71.4 36.2 %collective-permute-done.3 = bf16[2,2,2,1,1,24,3200]{6,5,4,3,2,1,0:T(8,128)(2,1)S(1)} collective-permute-done((bf16[2,2,2,1,1,24,3200]{6,5,4,3,2,1,0:T(8,128)(2,1)S(1)}, bf16[2,2,2,1,1,24,3200]{6,5,4,3,2,1,0:T(8,128)(2,1)S(1)}, u32[]{:S(2)}, u32[]{:S(2)}) %collective-permute-start.3) | collective-permute-done | bytes 1228832 | tf_op jit(solution)/shard_map/ppermute | solution.py:288
  108.7 3.4 constant_dynamic-slice_fusion.24
  117.3 3.4 constant_dynamic-update-slice_fusion
  122.9 4.5 %convolution_convert_fusion.query_ref.key_ref.value_ref.refs_1_.refs_2_.refs_3_ = bf16[4,128,2304]{2,1,0:T(8,128)(2,1)S(1)} fusion(bf16[768,3200]{1,0:T(8,128)(2,1)} %bitcast.116, f32[768]{0:T(1024)S(1)} %get-tuple-element.193, f32[768]{0:T(1024)S(1)} %get-tuple-element.194, f32[4,128]{1,0:T(4,128)S(1)} %add_rsqrt_fusion.2, ...), kind=kOutput, calls=%fused_computation.2 | convolution fusion | flops 1815478272 | bytes 6694912 | tf_op jit(solution)/shard_map/dot_general | solution.py:25
  127.4 4.5 %self_attention.1 = bf16[4,128,768]{2,1,0:T(8,128)(2,1)S(1)} custom-call(s32[4]{0:T(128)S(1)} %copy-done.10, bf16[4,128,2304]{2,1,0:T(8,128)(2,1)S(1)} %convolution_convert_fusion.query_ref.key_ref.value_ref.refs_1_.refs_2_.refs_3_, bf16[4,128,2304]{2,1,0:T(8,128)(2,1)S(1)} %convolution_convert_fusion.query_ref.key_ref.value_ref.refs_1_.refs_2_.refs_3_, ...), custom_call_target="tpu_custom_call" | custom-call | flops 201326592 | tf_op jit(solution)/shard_map/self_attention/pallas_call | solution.py:198
  139.9 3.0 all-gather.2.cloned.1.call-done.expand_ref.reduce_ref
  142.9 4.2 %convolution_convert_fusion.1.key_ref.value_ref = bf16[4,196,1536]{2,1,0:T(8,128)(2,1)S(1)} fusion(bf16[4,196,768]{2,1,0:T(8,128)(2,1)} %constant_dynamic-update-slice_fusion.6, bf16[768,9216]{1,0:T(8,128)(2,1)} %all-gather.2.cloned.1.call-done.expand_ref.reduce_ref), kind=kOutput, calls=%fused_computation.7 | convolution fusion | flops 1850892288 | bytes 5996544 | tf_op jit(solution)/shard_map/dot_general | solution.py:25
  147.1 3.1 convolution_convert_fusion.6.query_ref
  150.2 4.1 %cross_attention.1 = bf16[4,128,768]{2,1,0:T(8,128)(2,1)S(1)} custom-call(s32[4]{0:T(128)S(1)} %get-tuple-element.84.table_ref, bf16[4,128,768]{2,1,0:T(8,128)(2,1)S(1)} %convolution_convert_fusion.6.query_ref, bf16[4,196,1536]{2,1,0:T(8,128)(2,1)S(1)} %convolution_convert_fusion.1.key_ref.value_ref, ...), custom_call_target="tpu_custom_call" | custom-call | flops 308281344 | tf_op jit(solution)/shard_map/cross_attention/pallas_call | solution.py:198
  158.4 25.8 %ffn.1 = (f32[512,768]{1,0:T(8,128)S(1)}, f32[512,768]{1,0:T(8,128)S(1)}, bf16[3072,768]{1,0:T(8,128)(2,1)}, bf16[768,3072]{1,0:T(8,128)(2,1)}) custom-call(bf16[512,768]{1,0:T(8,128)(2,1)S(1)} %bitcast.110, bf16[512,768]{1,0:T(8,128)(2,1)S(1)} %bitcast.109, bf16[768,9216]{1,0:T(8,128)(2,1)} %all-gather.2.cloned.1.call-done.expand_ref.reduce_ref, ...), custom_call_target="tpu_custom_call" | custom-call | tf_op jit(solution)/shard_map/ffn/pallas_call | solution.py:103
  184.2 4.4 %constant_dynamic-slice_fusion.23 = bf16[2,2,2,2,1,96,768]{6,5,4,3,2,1,0:T(8,128)(2,1)} fusion(bf16[2,2,2,2,2,96,768]{6,5,4,3,2,1,0:T(8,128)(2,1)} %bitcast.127, s32[]{:T(128)S(6)} %select_n.225), kind=kLoop, calls=%fused_computation.127 | loop fusion | bytes 4718596 | tf_op jit(solution)/shard_map/dynamic_slice | solution.py:314
  207.4 11.8 %cross_backward.1 = (bf16[4,128,768]{2,1,0:T(8,128)(2,1)S(1)}, bf16[4,196,1536]{2,1,0:T(8,128)(2,1)S(1)}) custom-call(s32[4]{0:T(128)S(1)} %get-tuple-element.84.table_ref, bf16[4,128,768]{2,1,0:T(8,128)(2,1)S(1)} %copy-done.4, bf16[4,196,1536]{2,1,0:T(8,128)(2,1)} %copy-done, bf16[4,196,1536]{2,1,0:T(8,128)(2,1)} %copy-done, ...), custom_call_target="tpu_custom_call" | custom-call | flops 770703360 | tf_op jit(solution)/shard_map/cross_backward/pallas_call | solution.py:198
  219.3 4.5 %bitcast_convert_fusion.1 = bf16[768,1536]{1,0:T(8,128)(2,1)S(1)} fusion(bf16[4,196,768]{2,1,0:T(8,128)(2,1)} %constant_dynamic-update-slice_fusion.6, bf16[4,196,1536]{2,1,0:T(8,128)(2,1)S(1)} %get-tuple-element.96), kind=kOutput, calls=%fused_computation.1 | convolution fusion | flops 1850867712 | bytes 5971968 | tf_op jit(solution)/shard_map/dot_general | solution.py:39
  224.9 6.1 %fusion.21 = bf16[4,196,768]{2,1,0:T(8,128)(2,1)} fusion(bf16[4,196,1536]{2,1,0:T(8,128)(2,1)S(1)} %get-tuple-element.96, bf16[768,9216]{1,0:T(8,128)(2,1)} %all-gather.2.cloned.1.call-done.expand_ref.reduce_ref), kind=kOutput, calls=%fused_computation.58 | convolution fusion | flops 1850290176 | bytes 5971968 | tf_op jit(solution)/shard_map/dot_general | solution.py:32
  236.9 2.5 fusion.15
  251.7 3.6 bitcast_convert_fusion.3
  266.7 8.7 %self_backward.1 = bf16[4,128,2304]{2,1,0:T(8,128)(2,1)S(1)} custom-call(s32[4]{0:T(128)S(1)} %copy-done.10, bf16[4,128,2304]{2,1,0:T(8,128)(2,1)S(1)} %convolution_convert_fusion.query_ref.key_ref.value_ref.refs_1_.refs_2_.refs_3_, bf16[4,128,2304]{2,1,0:T(8,128)(2,1)S(1)} %convolution_convert_fusion.query_ref.key_ref.value_ref.refs_1_.refs_2_.refs_3_, ...), custom_call_target="tpu_custom_call" | custom-call | flops 503316480 | tf_op jit(solution)/shard_map/self_backward/pallas_call | solution.py:198
  276.5 8.3 %collective-permute-done.17 = bf16[2,2,1,2,1,24,2304]{6,5,4,3,2,1,0:T(8,128)(2,1)S(1)} collective-permute-done((bf16[2,2,1,2,1,24,2304]{6,5,4,3,2,1,0:T(8,128)(2,1)S(1)}, bf16[2,2,1,2,1,24,2304]{6,5,4,3,2,1,0:T(8,128)(2,1)S(1)}, u32[]{:S(2)}, u32[]{:S(2)}) %collective-permute-start.17) | collective-permute-done | bytes 884768 | tf_op jit(solution)/shard_map/ppermute | solution.py:324
  295.6 2.5 collective-permute-start.22
  317.1 3.6 collective-permute-start.28
  324.8 2.7 collective-permute-done.27
  329.8 9.4 %collective-permute-done.29 = bf16[2,2,1,2,1,24,1920]{6,5,4,3,2,1,0:T(8,128)(2,1)S(1)} collective-permute-done((bf16[2,2,1,2,1,24,1920]{6,5,4,3,2,1,0:T(8,128)(2,1)S(1)}, bf16[2,2,1,2,1,24,1920]{6,5,4,3,2,1,0:T(8,128)(2,1)S(1)}, u32[]{:S(2)}, u32[]{:S(2)}) %collective-permute-start.29) | collective-permute-done | bytes 737312 | tf_op jit(solution)/shard_map/ppermute | solution.py:324
  345.5 6.5 %collective-permute-done.31 = bf16[2,2,1,1,1,24,1920]{6,5,4,3,2,1,0:T(8,128)(2,1)S(1)} collective-permute-done((bf16[2,2,1,1,1,24,1920]{6,5,4,3,2,1,0:T(8,128)(2,1)S(1)}, bf16[2,2,1,1,1,24,1920]{6,5,4,3,2,1,0:T(8,128)(2,1)S(1)}, u32[]{:S(2)}, u32[]{:S(2)}) %collective-permute-start.31) | collective-permute-done | bytes 368672 | tf_op jit(solution)/shard_map/ppermute | solution.py:324
  352.3 3.5 collective-permute-start.35
  357.5 3.6 put_rows.1
  361.0 2.8 copy.77
  363.8 5.6 %collective-permute-done.33 = bf16[1,1,1,1,1,24,3968]{6,5,4,3,2,1,0:T(8,128)(2,1)S(1)} collective-permute-done((bf16[1,1,1,1,1,24,3968]{6,5,4,3,2,1,0:T(8,128)(2,1)S(1)}, bf16[1,1,1,1,1,24,3968]{6,5,4,3,2,1,0:T(8,128)(2,1)S(1)}, u32[]{:S(2)}, u32[]{:S(2)}) %collective-permute-start.33) | collective-permute-done | bytes 190496 | tf_op jit(solution)/shard_map/ppermute | solution.py:324
  (356 shorter events, 136.3 us)
Async XLA Ops:
  7.2 135.6 %all-gather.2.cloned.1.call-start = ((), (), s32[]{:S(2)}) async-start(), calls=%async_computation | async-start | bytes 14598144 | tf_op jit(solution)/shard_map/all_gather | solution.py:428
  10.8 11.4 %collective-permute-start = (bf16[1,1,1,1,1,24,3200]{6,5,4,3,2,1,0:T(8,128)(2,1)S(1)}, bf16[1,1,1,1,1,24,3200]{6,5,4,3,2,1,0:T(8,128)(2,1)S(1)}, u32[]{:S(2)}, u32[]{:S(2)}) collective-permute-start(bf16[1,1,1,1,1,24,3200]{6,5,4,3,2,1,0:T(8,128)(2,1)S(1)} %fusion.25), channel_id=1, source_target_pairs={{0,16},{4,20},{8,24},{12,28},{16,0},{20,4},{24,8},{28,12},{1,17},{... | collective-permute-start | bytes 460808 | tf_op jit(solution)/shard_map/ppermute | solution.py:288
  23.9 17.6 %collective-permute-start.1 = (bf16[2,1,1,1,1,24,3200]{6,5,4,3,2,1,0:T(8,128)(2,1)S(1)}, bf16[2,1,1,1,1,24,3200]{6,5,4,3,2,1,0:T(8,128)(2,1)S(1)}, u32[]{:S(2)}, u32[]{:S(2)}) collective-permute-start(bf16[2,1,1,1,1,24,3200]{6,5,4,3,2,1,0:T(8,128)(2,1)S(1)} %constant_dynamic-slice_fusion.31), channel_id=1, source_target_pairs={{0,8},{4,12},{8,0},{12,4},{16,24},{20,28},{24,16},{28,20},{1,9},{5... | collective-permute-start | bytes 921608 | tf_op jit(solution)/shard_map/ppermute | solution.py:288
  43.4 25.3 %collective-permute-start.2 = (bf16[2,2,1,1,1,24,3200]{6,5,4,3,2,1,0:T(8,128)(2,1)S(1)}, bf16[2,2,1,1,1,24,3200]{6,5,4,3,2,1,0:T(8,128)(2,1)S(1)}, u32[]{:S(2)}, u32[]{:S(2)}) collective-permute-start(bf16[2,2,1,1,1,24,3200]{6,5,4,3,2,1,0:T(8,128)(2,1)S(1)} %constant_dynamic-slice_fusion.26), channel_id=1, source_target_pairs={{0,4},{4,0},{8,12},{12,8},{16,20},{20,16},{24,28},{28,24},{1,5},{5... | collective-permute-start | bytes 1843208 | tf_op jit(solution)/shard_map/ppermute | solution.py:288
  70.9 36.7 %collective-permute-start.3 = (bf16[2,2,2,1,1,24,3200]{6,5,4,3,2,1,0:T(8,128)(2,1)S(1)}, bf16[2,2,2,1,1,24,3200]{6,5,4,3,2,1,0:T(8,128)(2,1)S(1)}, u32[]{:S(2)}, u32[]{:S(2)}) collective-permute-start(bf16[2,2,2,1,1,24,3200]{6,5,4,3,2,1,0:T(8,128)(2,1)S(1)} %constant_dynamic-slice_fusion.25), channel_id=1, source_target_pairs={{0,2},{1,3},{2,0},{3,1},{4,6},{5,7},{6,4},{7,5},{8,10},{9,11},{10,... | collective-permute-start | bytes 3686408 | tf_op jit(solution)/shard_map/ppermute | solution.py:288
  114.3 17.6 %collective-permute-start.4 = (bf16[1,196,768]{2,1,0:T(8,128)(2,1)S(1)}, bf16[1,196,768]{2,1,0:T(8,128)(2,1)S(1)}, u32[]{:S(2)}, u32[]{:S(2)}) collective-permute-start(bf16[1,196,768]{2,1,0:T(8,128)(2,1)S(1)} %copy-done.58), channel_id=1, source_target_pairs={{0,1},{1,0},{2,3},{3,2},{4,5},{5,4},{6,7},{7,6},{8,9},{9,8},{10,11... | collective-permute-start | bytes 903176 | tf_op jit(solution)/shard_map/ppermute | solution.py:350
  114.5 17.4 %collective-permute-start.5 = (bf16[1,196,768]{2,1,0:T(8,128)(2,1)S(1)}, bf16[1,196,768]{2,1,0:T(8,128)(2,1)S(1)}, u32[]{:S(2)}, u32[]{:S(2)}) collective-permute-start(bf16[1,196,768]{2,1,0:T(8,128)(2,1)S(1)} %copy-done.57), channel_id=1, source_target_pairs={{0,2},{1,3},{2,0},{3,1},{4,6},{5,7},{6,4},{7,5},{8,10},{9,11},{10,... | collective-permute-start | bytes 903176 | tf_op jit(solution)/shard_map/ppermute | solution.py:350
  114.9 18.4 %collective-permute-start.6 = (bf16[1,196,768]{2,1,0:T(8,128)(2,1)S(1)}, bf16[1,196,768]{2,1,0:T(8,128)(2,1)S(1)}, u32[]{:S(2)}, u32[]{:S(2)}) collective-permute-start(bf16[1,196,768]{2,1,0:T(8,128)(2,1)S(1)} %copy-done.56), channel_id=1, source_target_pairs={{0,3},{1,2},{2,1},{3,0},{4,7},{5,6},{6,5},{7,4},{8,11},{9,10},{10,... | collective-permute-start | bytes 903176 | tf_op jit(solution)/shard_map/ppermute | solution.py:350
  188.6 11.1 %collective-permute-start.8 = (bf16[2,2,2,2,1,96,768]{6,5,4,3,2,1,0:T(8,128)(2,1)}, bf16[2,2,2,2,1,96,768]{6,5,4,3,2,1,0:T(8,128)(2,1)}, u32[]{:S(2)}, u32[]{:S(2)}) collective-permute-start(bf16[2,2,2,2,1,96,768]{6,5,4,3,2,1,0:T(8,128)(2,1)} %constant_dynamic-slice_fusion.23), channel_id=1, source_target_pairs={{0,1},{1,0},{2,3},{3,2},{4,5},{5,4},{6,7},{7,6},{8,9},{9,8},{10,11... | collective-permute-start | bytes 7077896 | tf_op jit(solution)/shard_map/ppermute | solution.py:324
  190.5 11.3 %collective-permute-start.9 = (bf16[2,2,2,2,1,24,3072]{6,5,4,3,2,1,0:T(8,128)(2,1)}, bf16[2,2,2,2,1,24,3072]{6,5,4,3,2,1,0:T(8,128)(2,1)}, u32[]{:S(2)}, u32[]{:S(2)}) collective-permute-start(bf16[2,2,2,2,1,24,3072]{6,5,4,3,2,1,0:T(8,128)(2,1)} %constant_dynamic-slice_fusion.22), channel_id=1, source_target_pairs={{0,1},{1,0},{2,3},{3,2},{4,5},{5,4},{6,7},{7,6},{8,9},{9,8},{10,11... | collective-permute-start | bytes 7077896 | tf_op jit(solution)/shard_map/ppermute | solution.py:324
  205.0 28.4 %collective-permute-start.10 = (bf16[2,2,1,2,1,96,768]{6,5,4,3,2,1,0:T(8,128)(2,1)}, bf16[2,2,1,2,1,96,768]{6,5,4,3,2,1,0:T(8,128)(2,1)}, u32[]{:S(2)}, u32[]{:S(2)}) collective-permute-start(bf16[2,2,1,2,1,96,768]{6,5,4,3,2,1,0:T(8,128)(2,1)} %constant_dynamic-slice_fusion.21), channel_id=1, source_target_pairs={{0,4},{4,0},{8,12},{12,8},{16,20},{20,16},{24,28},{28,24},{1,5},{5... | collective-permute-start | bytes 3538952 | tf_op jit(solution)/shard_map/ppermute | solution.py:324
  206.2 28.6 %collective-permute-start.11 = (bf16[2,2,2,1,1,24,3072]{6,5,4,3,2,1,0:T(8,128)(2,1)}, bf16[2,2,2,1,1,24,3072]{6,5,4,3,2,1,0:T(8,128)(2,1)}, u32[]{:S(2)}, u32[]{:S(2)}) collective-permute-start(bf16[2,2,2,1,1,24,3072]{6,5,4,3,2,1,0:T(8,128)(2,1)} %constant_dynamic-slice_fusion.20), channel_id=1, source_target_pairs={{0,2},{1,3},{2,0},{3,1},{4,6},{5,7},{6,4},{7,5},{8,10},{9,11},{10,... | collective-permute-start | bytes 3538952 | tf_op jit(solution)/shard_map/ppermute | solution.py:324
  240.4 14.9 %collective-permute-start.12 = (bf16[2,2,1,1,1,96,768]{6,5,4,3,2,1,0:T(8,128)(2,1)}, bf16[2,2,1,1,1,96,768]{6,5,4,3,2,1,0:T(8,128)(2,1)}, u32[]{:S(2)}, u32[]{:S(2)}) collective-permute-start(bf16[2,2,1,1,1,96,768]{6,5,4,3,2,1,0:T(8,128)(2,1)} %constant_dynamic-slice_fusion.19), channel_id=1, source_target_pairs={{0,2},{1,3},{2,0},{3,1},{4,6},{5,7},{6,4},{7,5},{8,10},{9,11},{10,... | collective-permute-start | bytes 1769480 | tf_op jit(solution)/shard_map/ppermute | solution.py:324
  242.1 14.6 %collective-permute-start.13 = (bf16[2,2,1,1,1,24,3072]{6,5,4,3,2,1,0:T(8,128)(2,1)}, bf16[2,2,1,1,1,24,3072]{6,5,4,3,2,1,0:T(8,128)(2,1)}, u32[]{:S(2)}, u32[]{:S(2)}) collective-permute-start(bf16[2,2,1,1,1,24,3072]{6,5,4,3,2,1,0:T(8,128)(2,1)} %constant_dynamic-slice_fusion.18), channel_id=1, source_target_pairs={{0,4},{4,0},{8,12},{12,8},{16,20},{20,16},{24,28},{28,24},{1,5},{5... | collective-permute-start | bytes 1769480 | tf_op jit(solution)/shard_map/ppermute | solution.py:324
  244.4 13.5 %collective-permute-start.14 = (bf16[2,2,2,2,1,24,2304]{6,5,4,3,2,1,0:T(8,128)(2,1)}, bf16[2,2,2,2,1,24,2304]{6,5,4,3,2,1,0:T(8,128)(2,1)}, u32[]{:S(2)}, u32[]{:S(2)}) collective-permute-start(bf16[2,2,2,2,1,24,2304]{6,5,4,3,2,1,0:T(8,128)(2,1)} %constant_dynamic-slice_fusion.17), channel_id=1, source_target_pairs={{0,1},{1,0},{2,3},{3,2},{4,5},{5,4},{6,7},{7,6},{8,9},{9,8},{10,11... | collective-permute-start | bytes 5308424 | tf_op jit(solution)/shard_map/ppermute | solution.py:324
  259.8 15.7 %collective-permute-start.15 = (bf16[2,1,1,1,1,96,768]{6,5,4,3,2,1,0:T(8,128)(2,1)S(1)}, bf16[2,1,1,1,1,96,768]{6,5,4,3,2,1,0:T(8,128)(2,1)S(1)}, u32[]{:S(2)}, u32[]{:S(2)}) collective-permute-start(bf16[2,1,1,1,1,96,768]{6,5,4,3,2,1,0:T(8,128)(2,1)S(1)} %constant_dynamic-slice_fusion.16), channel_id=1, source_target_pairs={{0,8},{4,12},{8,0},{12,4},{16,24},{20,28},{24,16},{28,20},{1,9},{5... | collective-permute-start | bytes 884744 | tf_op jit(solution)/shard_map/ppermute | solution.py:324
  262.8 13.6 %collective-permute-start.16 = (bf16[2,1,1,1,1,24,3072]{6,5,4,3,2,1,0:T(8,128)(2,1)}, bf16[2,1,1,1,1,24,3072]{6,5,4,3,2,1,0:T(8,128)(2,1)S(1)}, u32[]{:S(2)}, u32[]{:S(2)}) collective-permute-start(bf16[2,1,1,1,1,24,3072]{6,5,4,3,2,1,0:T(8,128)(2,1)} %constant_dynamic-slice_fusion.15), channel_id=1, source_target_pairs={{0,8},{4,12},{8,0},{12,4},{16,24},{20,28},{24,16},{28,20},{1,9},{5... | collective-permute-start | bytes 884744 | tf_op jit(solution)/shard_map/ppermute | solution.py:324
  262.9 21.8 %collective-permute-start.17 = (bf16[2,2,1,2,1,24,2304]{6,5,4,3,2,1,0:T(8,128)(2,1)S(1)}, bf16[2,2,1,2,1,24,2304]{6,5,4,3,2,1,0:T(8,128)(2,1)S(1)}, u32[]{:S(2)}, u32[]{:S(2)}) collective-permute-start(bf16[2,2,1,2,1,24,2304]{6,5,4,3,2,1,0:T(8,128)(2,1)S(1)} %constant_dynamic-slice_fusion.14), channel_id=1, source_target_pairs={{0,4},{4,0},{8,12},{12,8},{16,20},{20,16},{24,28},{28,24},{1,5},{5... | collective-permute-start | bytes 2654216 | tf_op jit(solution)/shard_map/ppermute | solution.py:324
  265.7 19.2 %collective-permute-start.18 = (bf16[1,196,768]{2,1,0:T(8,128)(2,1)S(1)}, bf16[1,196,768]{2,1,0:T(8,128)(2,1)S(1)}, u32[]{:S(2)}, u32[]{:S(2)}) collective-permute-start(bf16[1,196,768]{2,1,0:T(8,128)(2,1)S(1)} %get-tuple-element.203), channel_id=1, source_target_pairs={{0,1},{1,0},{2,3},{3,2},{4,5},{5,4},{6,7},{7,6},{8,9},{9,8},{10,11... | collective-permute-start | bytes 903176 | tf_op jit(solution)/shard_map/ppermute | solution.py:350
  265.7 19.2 %collective-permute-start.19 = (bf16[1,196,768]{2,1,0:T(8,128)(2,1)S(1)}, bf16[1,196,768]{2,1,0:T(8,128)(2,1)S(1)}, u32[]{:S(2)}, u32[]{:S(2)}) collective-permute-start(bf16[1,196,768]{2,1,0:T(8,128)(2,1)S(1)} %get-tuple-element.202), channel_id=1, source_target_pairs={{0,2},{1,3},{2,0},{3,1},{4,6},{5,7},{6,4},{7,5},{8,10},{9,11},{10,... | collective-permute-start | bytes 903176 | tf_op jit(solution)/shard_map/ppermute | solution.py:350
  275.5 9.5 %collective-permute-start.20 = (bf16[1,196,768]{2,1,0:T(8,128)(2,1)S(1)}, bf16[1,196,768]{2,1,0:T(8,128)(2,1)S(1)}, u32[]{:S(2)}, u32[]{:S(2)}) collective-permute-start(bf16[1,196,768]{2,1,0:T(8,128)(2,1)S(1)} %get-tuple-element.201), channel_id=1, source_target_pairs={{0,3},{1,2},{2,1},{3,0},{4,7},{5,6},{6,5},{7,4},{8,11},{9,10},{10,... | collective-permute-start | bytes 903176 | tf_op jit(solution)/shard_map/ppermute | solution.py:350
  293.9 19.8 %collective-permute-start.21 = (bf16[2,2,1,1,1,24,2304]{6,5,4,3,2,1,0:T(8,128)(2,1)}, bf16[2,2,1,1,1,24,2304]{6,5,4,3,2,1,0:T(8,128)(2,1)}, u32[]{:S(2)}, u32[]{:S(2)}) collective-permute-start(bf16[2,2,1,1,1,24,2304]{6,5,4,3,2,1,0:T(8,128)(2,1)} %constant_dynamic-slice_fusion.13), channel_id=1, source_target_pairs={{0,2},{1,3},{2,0},{3,1},{4,6},{5,7},{6,4},{7,5},{8,10},{9,11},{10,... | collective-permute-start | bytes 1327112 | tf_op jit(solution)/shard_map/ppermute | solution.py:324
  295.6 17.2 %collective-permute-start.22 = (bf16[1,1,1,1,1,96,768]{6,5,4,3,2,1,0:T(8,128)(2,1)}, bf16[1,1,1,1,1,96,768]{6,5,4,3,2,1,0:T(8,128)(2,1)}, u32[]{:S(2)}, u32[]{:S(2)}) collective-permute-start(bf16[1,1,1,1,1,96,768]{6,5,4,3,2,1,0:T(8,128)(2,1)} %constant_dynamic-slice_fusion.12), channel_id=1, source_target_pairs={{0,16},{4,20},{8,24},{12,28},{16,0},{20,4},{24,8},{28,12},{1,17},{... | collective-permute-start | bytes 442376 | tf_op jit(solution)/shard_map/ppermute | solution.py:324
  298.8 13.1 %collective-permute-start.23 = (bf16[1,1,1,1,1,24,3072]{6,5,4,3,2,1,0:T(8,128)(2,1)}, bf16[1,1,1,1,1,24,3072]{6,5,4,3,2,1,0:T(8,128)(2,1)}, u32[]{:S(2)}, u32[]{:S(2)}) collective-permute-start(bf16[1,1,1,1,1,24,3072]{6,5,4,3,2,1,0:T(8,128)(2,1)} %constant_dynamic-slice_fusion.11), channel_id=1, source_target_pairs={{0,16},{4,20},{8,24},{12,28},{16,0},{20,4},{24,8},{28,12},{1,17},{... | collective-permute-start | bytes 442376 | tf_op jit(solution)/shard_map/ppermute | solution.py:324
  302.2 12.7 %collective-permute-start.24 = (bf16[2,2,2,2,1,24,1920]{6,5,4,3,2,1,0:T(8,128)(2,1)}, bf16[2,2,2,2,1,24,1920]{6,5,4,3,2,1,0:T(8,128)(2,1)}, u32[]{:S(2)}, u32[]{:S(2)}) collective-permute-start(bf16[2,2,2,2,1,24,1920]{6,5,4,3,2,1,0:T(8,128)(2,1)} %constant_dynamic-slice_fusion.10), channel_id=1, source_target_pairs={{0,1},{1,0},{2,3},{3,2},{4,5},{5,4},{6,7},{7,6},{8,9},{9,8},{10,11... | collective-permute-start | bytes 4423688 | tf_op jit(solution)/shard_map/ppermute | solution.py:324
  307.5 9.0 %collective-permute-start.25 = (bf16[2,2,2,2,1,24,2048]{6,5,4,3,2,1,0:T(8,128)(2,1)S(1)}, bf16[2,2,2,2,1,24,2048]{6,5,4,3,2,1,0:T(8,128)(2,1)S(1)}, u32[]{:S(2)}, u32[]{:S(2)}) collective-permute-start(bf16[2,2,2,2,1,24,2048]{6,5,4,3,2,1,0:T(8,128)(2,1)S(1)} %fusion.16), channel_id=1, source_target_pairs={{0,1},{1,0},{2,3},{3,2},{4,5},{5,4},{6,7},{7,6},{8,9},{9,8},{10,11... | collective-permute-start | bytes 4718600 | tf_op jit(solution)/shard_map/ppermute | solution.py:324
  320.7 9.1 %collective-permute-start.26 = (bf16[1,1,1,1,1,24,2304]{6,5,4,3,2,1,0:T(8,128)(2,1)S(1)}, bf16[1,1,1,1,1,24,2304]{6,5,4,3,2,1,0:T(8,128)(2,1)S(1)}, u32[]{:S(2)}, u32[]{:S(2)}) collective-permute-start(bf16[1,1,1,1,1,24,2304]{6,5,4,3,2,1,0:T(8,128)(2,1)S(1)} %get-tuple-element.214), channel_id=1, source_target_pairs={{0,16},{4,20},{8,24},{12,28},{16,0},{20,4},{24,8},{28,12},{1,17},{... | collective-permute-start | bytes 331784 | tf_op jit(solution)/shard_map/ppermute | solution.py:324
  321.6 17.6 %collective-permute-start.29 = (bf16[2,2,1,2,1,24,1920]{6,5,4,3,2,1,0:T(8,128)(2,1)S(1)}, bf16[2,2,1,2,1,24,1920]{6,5,4,3,2,1,0:T(8,128)(2,1)S(1)}, u32[]{:S(2)}, u32[]{:S(2)}) collective-permute-start(bf16[2,2,1,2,1,24,1920]{6,5,4,3,2,1,0:T(8,128)(2,1)S(1)} %constant_dynamic-slice_fusion.6), channel_id=1, source_target_pairs={{0,4},{4,0},{8,12},{12,8},{16,20},{20,16},{24,28},{28,24},{1,5},{5... | collective-permute-start | bytes 2211848 | tf_op jit(solution)/shard_map/ppermute | solution.py:324
  322.7 18.4 %collective-permute-start.30 = (bf16[2,2,2,1,1,24,2048]{6,5,4,3,2,1,0:T(8,128)(2,1)S(1)}, bf16[2,2,2,1,1,24,2048]{6,5,4,3,2,1,0:T(8,128)(2,1)S(1)}, u32[]{:S(2)}, u32[]{:S(2)}) collective-permute-start(bf16[2,2,2,1,1,24,2048]{6,5,4,3,2,1,0:T(8,128)(2,1)S(1)} %constant_dynamic-slice_fusion.5), channel_id=1, source_target_pairs={{0,2},{1,3},{2,0},{3,1},{4,6},{5,7},{6,4},{7,5},{8,10},{9,11},{10,... | collective-permute-start | bytes 2359304 | tf_op jit(solution)/shard_map/ppermute | solution.py:324
  342.5 9.5 %collective-permute-start.32 = (bf16[2,2,1,1,1,24,2048]{6,5,4,3,2,1,0:T(8,128)(2,1)S(1)}, bf16[2,2,1,1,1,24,2048]{6,5,4,3,2,1,0:T(8,128)(2,1)S(1)}, u32[]{:S(2)}, u32[]{:S(2)}) collective-permute-start(bf16[2,2,1,1,1,24,2048]{6,5,4,3,2,1,0:T(8,128)(2,1)S(1)} %constant_dynamic-slice_fusion.3), channel_id=1, source_target_pairs={{0,4},{4,0},{8,12},{12,8},{16,20},{20,16},{24,28},{28,24},{1,5},{5... | collective-permute-start | bytes 1179656 | tf_op jit(solution)/shard_map/ppermute | solution.py:324
  352.3 11.5 %collective-permute-start.35 = (bf16[1,1,1,1,1,24,3968]{6,5,4,3,2,1,0:T(8,128)(2,1)S(1)}, bf16[1,1,1,1,1,24,3968]{6,5,4,3,2,1,0:T(8,128)(2,1)S(1)}, u32[]{:S(2)}, u32[]{:S(2)}) collective-permute-start(bf16[1,1,1,1,1,24,3968]{6,5,4,3,2,1,0:T(8,128)(2,1)S(1)} %get-tuple-element.212), channel_id=1, source_target_pairs={{0,24},{4,28},{8,16},{12,20},{16,8},{20,12},{24,0},{28,4},{1,25},{... | collective-permute-start | bytes 571400 | tf_op jit(solution)/shard_map/ppermute | solution.py:324
  355.7 13.7 %collective-permute-start.33 = (bf16[1,1,1,1,1,24,3968]{6,5,4,3,2,1,0:T(8,128)(2,1)S(1)}, bf16[1,1,1,1,1,24,3968]{6,5,4,3,2,1,0:T(8,128)(2,1)S(1)}, u32[]{:S(2)}, u32[]{:S(2)}) collective-permute-start(bf16[1,1,1,1,1,24,3968]{6,5,4,3,2,1,0:T(8,128)(2,1)S(1)} %get-tuple-element.211), channel_id=1, source_target_pairs={{0,16},{4,20},{8,24},{12,28},{16,0},{20,4},{24,8},{28,12},{1,17},{... | collective-permute-start | bytes 571400 | tf_op jit(solution)/shard_map/ppermute | solution.py:324
  (84 other events, 399.5 us)
Sparse Core Ops, SparseCore 0:
  11.5 131.3 all-gather.1
